TPU v7x, 1024 devices: a whole 4x8x16 slice. The times are simulated.
1024 devices in a mesh: seq: 128 (over z, x, core), head: 8 (over y).
Axes of the slice: x: 4, y: 8, z: 16, core: 2. Of those that a mesh axis runs over, the one named last changes fastest.
Arguments:
- grad_out: bfloat16 [16384, 3072], P('seq', 'head'), may hold values from -6 to 6
- out_weight: bfloat16 [3072, 3072], P('head', 'seq'), may hold values from -0.109375 to 0.109375
- row_owner: int32 [16384], P('seq'), may hold values from 0 to 127, as said below
- row_position: int32 [16384], P('seq'), may hold values from 0 to 127, as said below
- query_rows: bfloat16 [16384, 3072], P('seq', 'head'), may hold values from -48 to 48
- key_rows: bfloat16 [16384, 3072], P('seq', 'head'), may hold values from -48 to 48
- value_rows: bfloat16 [16384, 3072], P('seq', 'head'), may hold values from -6 to 6
- band_widths: int32 [128, 2], P('seq'), may hold values from 16 to 64, as said below
Outputs:
- grad_query: bfloat16 [16384, 3072], P('seq', 'head')
- grad_key: bfloat16 [16384, 3072], P('seq', 'head')
- grad_value: bfloat16 [16384, 3072], P('seq', 'head')
Inputs may be any that keep to these rules, and one draw needn't show every extreme that they name: `row_owner`: each frame receives each of its 128 positions from exactly one packed row. One device holds at most 1 row of one frame, and every device holds exactly 1 row of some frame; how many rows device s holds of frame o depends only on (o - s) mod 128, and is at least one for (o - s) mod 128 equal to 1, 64 and 127. `row_position`: together with row_owner, a permutation of all tokens. `band_widths`: column 0 lies in 32 to 64, column 1 in 16 to 32.
All inputs are finite; a program needn't handle non-finite values.
Results may differ from a plain program's by a relative error of at most 0.0088.
Values may be sent and summed in bfloat16 or wider, within the bound.
No kernel may reach another device: no remote copies, remote signals or barrier semaphores. Data moves between devices by JAX's collectives and lax.ppermute only.
A program may use at most 32 MiB of HBM per device.

v0:
```python
import functools

import jax
import jax.numpy as jnp
from jax import lax
from jax.experimental import pallas as pl
from jax.experimental.pallas import tpu as pltpu
from jax.sharding import Mesh
from jax.sharding import PartitionSpec as P


HEAD_DIM = 128
LANES = 128
DISTANCES = (0, 1, 2, 4)
NEG_FILL = -1e30
SEQ = ("z", "x", "core")
SIZES = {"z": 16, "x": 4, "core": 2}
F32 = jnp.float32
BF16 = jnp.bfloat16
SCALE = HEAD_DIM ** (-0.5)


def shifted(value, by):
    peers = lax.axis_size(SEQ)
    pairs = [(i, i + by) for i in range(peers) if 0 <= i + by < peers]
    return lax.ppermute(value, SEQ, pairs)


def turned(value, axis, by):
    peers = lax.axis_size(axis)
    return lax.ppermute(value, axis, [(i, (i + by) % peers) for i in range(peers)])


def exchange(value, axis):
    return lax.all_to_all(value, axis, split_axis=0, concat_axis=0, tiled=True)


def dot(a, b, left, right):
    return lax.dot_general(a, b, (((left,), (right,)), ((), ())), preferred_element_type=F32)


SPACES = {"s": pltpu.SMEM, "v": pltpu.VMEM, "h": pltpu.HBM}


def call(body, outs, spaces, args, flops, scratch=(), copies=0):
    specs = [pl.BlockSpec(memory_space=SPACES[c]) for c in spaces]
    size = sum(a.size * a.dtype.itemsize for a in args)
    size += sum(int(jnp.dtype(t).itemsize) * functools.reduce(lambda m, n: m * n, s) for s, t in outs)
    args = [pltpu.with_memory_space_constraint(a, pltpu.HBM) if c == "h" else a for a, c in zip(args, spaces)]
    scratch = [pltpu.VMEM(shape, kind) for shape, kind in scratch]
    if copies:
        scratch.append(pltpu.SemaphoreType.DMA((copies,)))
    return pl.pallas_call(
        body,
        out_shape=[
            pltpu.HBM(s, t) if c == "h" else jax.ShapeDtypeStruct(s, t)
            for (s, t), c in zip(outs, spaces[len(args) :])
        ],
        in_specs=specs[: len(args)],
        out_specs=specs[len(args) :],
        scratch_shapes=scratch,
        cost_estimate=pl.CostEstimate(flops=flops, bytes_accessed=size, transcendentals=0),
        compiler_params=pltpu.CompilerParams(vmem_limit_bytes=8 * 2**20),
    )(*args)


def started(pairs, sems):
    copies = [pltpu.make_async_copy(a, b, sems.at[i]) for i, (a, b) in enumerate(pairs)]
    for copy in copies:
        copy.start()
    return copies


def wait(copies):
    for copy in copies:
        copy.wait()


def iota(shape, dim):
    return lax.broadcasted_iota(jnp.int32, shape, dim)


def lanes(h):
    return slice(h * LANES, (h + 1) * LANES)


def pack_body(frame, owner_h, place_h, grad_h, weight_h, key_h, value_h, out, pair, owner, place, grad, weight, sems):
    moves = ((owner_h, owner), (place_h, place), (grad_h, grad), (weight_h, weight))
    moves += ((key_h, pair.at[:, :384]), (value_h, pair.at[:, 384:]))
    copies = started(moves, sems)
    wait(copies[:4])
    pick = iota((128, 128), 0) == owner[...]
    where = jnp.sum(jnp.where(pick, place[...].astype(F32), 0.0), axis=1, keepdims=True)
    where = jnp.broadcast_to(where, (128, LANES)).astype(BF16)
    rows = dot(pick.astype(BF16), grad[...], 1, 0).astype(BF16)
    for h in range(3):
        piece = weight[:, lanes(h)]
        for z in range(16):
            out[z, 24 * h : 24 * h + 24, :] = piece
            out[z, 72 + 8 * h : 80 + 8 * h, :] = rows[8 * z : 8 * z + 8, lanes(h)]
    for z in range(16):
        out[z, 96:104, :] = where[8 * z : 8 * z + 8]
    wait(copies[4:])


def split_body(got, weight, rows, sems):
    copies = started(((got.at[:, :72, :], weight),), sems)
    row, col = iota((128, 128), 0), iota((128, 128), 1)
    order = (col == (row & 15) * 8 + (row >> 4)).astype(BF16)
    blocks = [
        dot(order, got[:, 72 + 8 * b : 80 + 8 * b, :].reshape(128, LANES), 1, 0) for b in range(4)
    ]
    cell = iota((1, 512), 1)
    at = cell & 255
    source = ((at * 2731) >> 16) * 24 + at + (cell >> 8) * 24
    source = jnp.where(at < 192, source, -1)
    move = (iota((384, 512), 0) == source).astype(BF16)
    sorted_rows = dot(jnp.concatenate(blocks[:3], axis=1).astype(BF16), move, 1, 0)
    tag = jnp.where(iota((128, 256), 1) >= 192, jnp.concatenate([blocks[3]] * 2, axis=1), 0.0)
    for core in range(2):
        half = (sorted_rows[:, 256 * core : 256 * core + 256] + tag).astype(BF16)
        for x in range(4):
            rows[2 * x + core] = half[32 * x : 32 * x + 32]
    wait(copies)


def land_body(got, out):
    total = None
    to = iota((1, 384), 1)
    for c in range(2):
        flat = got[:, 16 * c : 16 * c + 16, :].reshape(128, 256)
        where = flat[:, 192:193].astype(F32) == iota((128, 128), 1).astype(F32)
        rows = dot(where.astype(BF16), flat, 0, 0).astype(BF16)
        first, second = to - 128 * c, to - 128 - 64 * c
        source = jnp.where(
            (first >= 0) & (first < 128), first, jnp.where((second >= 128) & (second < 192), second, -1)
        )
        part = dot(rows, (iota((256, 384), 0) == source).astype(BF16), 1, 0)
        total = part if total is None else total + part
    total = total.astype(BF16)
    for y in range(8):
        out[y] = total


def forward_body(
    frame, band, query_h, key_h, value_h, b1, b2, b4, l1, l2, l4, prob_h, norm_h, score_h,
    query, key, pairs, later, prob, norm, score, sems
):
    moves = [(query_h, query), (key_h, key)]
    moves += [(b.at[:, :384], pairs.at[i]) for i, b in enumerate((b1, b2, b4))]
    moves += [(b, later.at[i]) for i, b in enumerate((l1, l2, l4))]
    wait(started(moves, sems))
    spread = jnp.abs(iota((128, 128), 0) - iota((128, 128), 1))
    f = frame[0]
    limits = [
        None,
        jnp.where(f >= 1, 128, 0),
        jnp.where(f >= 2, band[0, 0], 0),
        jnp.where(f >= 4, band[0, 1], 0),
    ]
    for h in range(3):
        q = query[:, lanes(h)]
        parts = []
        for i, limit in enumerate(limits):
            keys = key[:, lanes(h)] if i == 0 else pairs[i - 1, :, lanes(h)]
            s = dot(keys, q, 1, 1) * SCALE
            parts.append(s if limit is None else jnp.where(spread < limit, s, NEG_FILL))
        s = jnp.concatenate(parts, axis=0)
        top = jnp.max(s, axis=0, keepdims=True)
        w = jnp.exp(s - top)
        total = jnp.sum(w, axis=0, keepdims=True)
        prob[h] = w / total
        norm[:, lanes(h)] = jnp.broadcast_to(top + jnp.log(total), (8, 128))
        for i in range(3):
            score[3 * i + h] = dot(key[:, lanes(h)], later[i, :, lanes(h)], 1, 1) * SCALE
    wait(started(((prob, prob_h), (norm, norm_h), (score, score_h)), sems))


def parts_of(value):
    high = value.astype(BF16)
    rest = value - high.astype(F32)
    middle = rest.astype(BF16)
    return high, middle, (rest - middle.astype(F32)).astype(BF16)


def project_body(
    frame, rows, o0, o1, o2, o3, key_h, value_h, b1, b2, b4, prob_h, norm_h,
    mine, yours, keys, values, prob, norm, weight, sems
):
    x, core = (frame[0] >> 1) & 3, frame[0] & 1
    moves = []
    for turn, piece in enumerate((o0, o1, o2, o3)):
        to_x = (x + 4 - turn) & 3
        for h in range(3):
            moves.append((piece.at[:, 24 * h : 24 * h + 24, :], weight.at[:, to_x, :, lanes(h)]))
    moves += [(key_h, keys.at[0]), (value_h, values.at[0]), (prob_h, prob), (norm_h, norm)]
    for i, pair in enumerate((b1, b2, b4)):
        moves += [(pair.at[:, :384], keys.at[i + 1]), (pair.at[:, 384:], values.at[i + 1])]
    copies = started(moves, sems)
    wait(copies[:12])
    low = (iota((128, 128), 1) < 64).astype(F32).astype(BF16)
    high = (iota((128, 128), 1) >= 64).astype(F32).astype(BF16)
    total = None
    for y in range(8):
        block = rows[y]
        both = [
            jnp.concatenate([block[:, lanes(c)], block[:, 256:] * side], axis=1)
            for c, side in enumerate((low, high))
        ]
        block = weight[2 * y : 2 * y + 2].reshape(192, 384)
        block = jnp.concatenate([block, block[128:]], axis=0)
        part = dot(jnp.concatenate(both, axis=0), block, 1, 0)
        total = part if total is None else total + part
    mine[...] = jnp.where(core == 0, total[:128], total[128:])
    yours[...] = jnp.where(core == 0, total[128:], total[:128])
    wait(copies[12:])


def finish_body(band, mine, other, values, prob, norm, parcel, row_dot):
    grad = (mine[...] + other[...]).astype(BF16)
    parcel[:128, :] = grad
    dots = []
    for h in range(3):
        g = grad[:, lanes(h)]
        whole = jnp.zeros((1, 128), F32)
        for i in range(4):
            p = prob[h, 128 * i : 128 * i + 128].astype(BF16).astype(F32)
            whole = whole + jnp.sum(p * dot(values[i, :, lanes(h)], g, 1, 1), axis=0, keepdims=True)
        dots.append(whole)
    dots = jnp.concatenate(dots, axis=1)
    row_dot[...] = jnp.broadcast_to(dots, (8, 384))
    bands = [jnp.full((1, 384), band[0, i], jnp.int32).astype(F32) for i in range(2)]
    stack = [v.astype(F32) for v in parts_of(norm[:1]) + parts_of(dots)] + bands
    parcel[128:, :] = jnp.concatenate(stack, axis=0).astype(BF16)


def own_body(
    parcel, row_dot, prob, query_h, keys, values, l1, l2, l4, score_h,
    grad_query, key_part, value_part, later, score, query, sems
):
    moves = [(query_h, query), (score_h, score)]
    moves += [(b, later.at[i]) for i, b in enumerate((l1, l2, l4))]
    copies = started(moves, sems)
    for h in range(3):
        g = parcel[:128, lanes(h)]
        total = None
        for i in range(4):
            p = prob[h, 128 * i : 128 * i + 128]
            s = p * (dot(values[i, :, lanes(h)], g, 1, 1) - row_dot[:1, lanes(h)])
            s = s.astype(BF16)
            part = dot(s, keys[i, :, lanes(h)], 0, 0)
            total = part if total is None else total + part
            if i == 0:
                if h == 0:
                    wait(copies[:1])
                key_part[:, lanes(h)] = dot(s, query[:, lanes(h)], 1, 0)
                value_part[:, lanes(h)] = dot(p.astype(BF16), g, 1, 0)
        grad_query[:, lanes(h)] = (SCALE * total).astype(BF16)
    wait(copies[1:])


def later_body(frame, a1, a2, a4, later, score, values, key_part, value_part, grad_key, grad_value):
    spread = jnp.abs(iota((128, 128), 0) - iota((128, 128), 1)).astype(F32)
    for h in range(3):
        keys, vals = key_part[:, lanes(h)], value_part[:, lanes(h)]
        for i, (d, box) in enumerate(((1, a1), (2, a2), (4, a4))):
            extra = box[128:, lanes(h)].astype(F32)
            norm = extra[0:1] + extra[1:2] + extra[2:3]
            row_dot = extra[3:4] + extra[4:5] + extra[5:6]
            limit = jnp.full((1, 128), 128.0, F32) if d == 1 else extra[5 + d // 2 : 6 + d // 2]
            limit = jnp.where(frame[0] + d < 128, limit, 0.0)
            p = jnp.where(spread < limit, jnp.exp(score[3 * i + h] - norm), 0.0)
            g = box[:128, lanes(h)]
            s = (p * (dot(values[0, :, lanes(h)], g, 1, 1) - row_dot)).astype(BF16)
            keys = keys + dot(s, later[i, :, lanes(h)], 1, 0)
            vals = vals + dot(p.astype(BF16), g, 1, 0)
        grad_key[:, lanes(h)] = (SCALE * keys).astype(BF16)
        grad_value[:, lanes(h)] = vals.astype(BF16)


def step(
    grad_out, out_weight, row_owner, row_position, query_rows, key_rows, value_rows, band_widths
):
    frame = lax.axis_index(SEQ).reshape(1)

    packed, pair = call(
        pack_body,
        [((16, 104, LANES), BF16), ((128, 768), BF16)],
        "s" + "h" * 6 + "vv",
        (frame, row_owner[None], row_position[None], grad_out, out_weight.T, key_rows, value_rows),
        13_000_000,
        [((1, 128), jnp.int32), ((1, 128), jnp.int32), ((128, 384), BF16), ((24, 384), BF16)],
        6,
    )
    got = exchange(packed, "z")
    pairs, later = [], []
    for d in DISTANCES[1:]:
        pairs.append(shifted(pair, d))
    for d in DISTANCES[1:]:
        later.append(shifted(query_rows, -d))
    got, *later = lax.optimization_barrier((got, *later))
    own, rows = call(split_body, [((16, 72, LANES), BF16), ((8, 32, 256), BF16)], "vhv", (got,), 70_000_000, (), 1)
    rows = exchange(rows, ("x", "core"))
    (rows,) = call(land_body, [((8, 128, 384), BF16)], "vv", (rows,), 13_000_000)
    rows = exchange(rows, "head")

    right = turned(own, "x", 1)
    left = turned(own, "x", -1)
    far = turned(right, "x", 1)
    prob, norm, score = call(
        forward_body,
        [((3, 512, 128), F32), ((8, 384), F32), ((9, 128, 128), F32)],
        "ss" + "h" * 12,
        (frame, band_widths, query_rows, key_rows, value_rows, *pairs, *later),
        90_000_000,
        [((128, 384), BF16), ((128, 384), BF16), ((3, 128, 384), BF16), ((3, 128, 384), BF16)]
        + [((3, 512, 128), F32), ((8, 384), F32), ((9, 128, 128), F32)],
        8,
    )
    rows, far, left, prob, norm, score = lax.optimization_barrier((rows, far, left, prob, norm, score))

    mine, yours, keys, values, prob, norm = call(
        project_body,
        [((128, 384), F32)] * 2 + [((4, 128, 384), BF16)] * 2 + [((3, 512, 128), F32), ((8, 384), F32)],
        "sv" + "h" * 11 + "v" * 6,
        (frame, rows, own, right, far, left, key_rows, value_rows, *pairs, prob, norm),
        350_000_000,
        [((16, 4, 24, 384), BF16)],
        22,
    )
    other = turned(yours, "core", 1)
    parcel, row_dot = call(
        finish_body,
        [((136, 384), BF16), ((8, 384), F32)],
        "s" + "v" * 7,
        (band_widths, mine, other, values, prob, norm),
        50_000_000,
    )
    boxes = []
    for d in DISTANCES[1:]:
        boxes.append(shifted(parcel, -d))
    grad_query, key_part, value_part, later, score = call(
        own_body,
        [((128, 384), BF16), ((128, 384), F32), ((128, 384), F32), ((3, 128, 384), BF16), ((9, 128, 128), F32)],
        "vvvhvvhhhh" + "v" * 5,
        (parcel, row_dot, prob, query_rows, keys, values, *later, score),
        120_000_000,
        [((128, 384), BF16)],
        5,
    )
    grad_key, grad_value = call(
        later_body,
        [((128, 384), BF16), ((128, 384), BF16)],
        "s" + "v" * 10,
        (frame, *boxes, later, score, values, key_part, value_part),
        120_000_000,
    )
    return grad_query, grad_key, grad_value


def solution(mesh):
    grid = mesh.devices.reshape(tuple(SIZES.values()) + (mesh.shape["head"],))
    fine = Mesh(grid, tuple(SIZES) + ("head",))
    return jax.shard_map(
        step,
        mesh=fine,
        in_specs=(
            P(SEQ, "head"),
            P("head", SEQ),
            P(SEQ),
            P(SEQ),
            P(SEQ, "head"),
            P(SEQ, "head"),
            P(SEQ, "head"),
            P(SEQ, None),
        ),
        out_specs=(P(SEQ, "head"), P(SEQ, "head"), P(SEQ, "head")),
        check_vma=False,
    )
```

profile of v0, /device:TPU:7, one launch (start us, length us, event | category | flops | bytes accessed | tf_op | source)
XLA Modules:
  0.0 124.1 jit_solution(6925395613252565641)
XLA Ops:
  0.6 1.9 %shard_map.103 = (bf16[16,104,128]{2,1,0:T(8,128)(2,1)}, bf16[128,768]{1,0:T(8,128)(2,1)S(1)}) custom-call(s32[1]{0:T(128)} %bitcast.frame, s32[1,128]{1,0:T(1,128)} %bitcast.5, s32[1,128]{1,0:T(1,128)} %bitcast.6, bf16[128,384]{1,0:T(8,128)(2,1)} %grad_h.1, bf16[24,384]{1,0:T(8,128)(2,1)} %bitcast.4, bf16[128,384]{1,0:T(8,128)(2,1)} %key_h.5, ...), custom_call_target="tpu_custom_call" | custom-call | flops 13000000 | bytes 936964 | tf_op jit(solution)/shard_map/pallas_call | solution.py:53
  2.6 0.0 copy-start.4
  2.6 18.7 %all-to-all-start = ((bf16[16,104,128]{2,1,0:T(8,128)(2,1)}), bf16[16,104,128]{2,1,0:T(8,128)(2,1)S(1)}, u32[]{:S(2)}, u32[]{:S(2)}) async-start(bf16[16,104,128]{2,1,0:T(8,128)(2,1)} %get-tuple-element.35), calls=%async_computation | async-start | bytes 851968 | tf_op jit(solution)/shard_map/all_to_all | solution.py:35
  21.3 0.0 copy-done.4
  21.3 3.0 %collective-permute-start.2 = (bf16[128,384]{1,0:T(8,128)(2,1)S(1)}, bf16[128,384]{1,0:T(8,128)(2,1)S(1)}, u32[]{:S(2)}, u32[]{:S(2)}) collective-permute-start(bf16[128,384]{1,0:T(8,128)(2,1)S(1)} %copy-done.4), channel_id=1, source_target_pairs={{32,0},{40,8},{48,16},{56,24},{64,32},{72,40},{80,48},{88,56},{96,... | collective-permute-start | bytes 294920 | tf_op jit(solution)/shard_map/ppermute | solution.py:26
  24.4 1.9 %collective-permute-start.1 = (bf16[128,384]{1,0:T(8,128)(2,1)S(1)}, bf16[128,384]{1,0:T(8,128)(2,1)S(1)}, u32[]{:S(2)}, u32[]{:S(2)}) collective-permute-start(bf16[128,384]{1,0:T(8,128)(2,1)S(1)} %copy-done.4), channel_id=1, source_target_pairs={{16,0},{24,8},{32,16},{40,24},{48,32},{56,40},{64,48},{72,56},{80,... | collective-permute-start | bytes 294920 | tf_op jit(solution)/shard_map/ppermute | solution.py:26
  26.3 3.1 %collective-permute-start = (bf16[128,384]{1,0:T(8,128)(2,1)S(1)}, bf16[128,384]{1,0:T(8,128)(2,1)S(1)}, u32[]{:S(2)}, u32[]{:S(2)}) collective-permute-start(bf16[128,384]{1,0:T(8,128)(2,1)S(1)} %copy-done.4), channel_id=1, source_target_pairs={{8,0},{16,8},{24,16},{32,24},{40,32},{48,40},{56,48},{64,56},{72,6... | collective-permute-start | bytes 294920 | tf_op jit(solution)/shard_map/ppermute | solution.py:26
  29.5 14.7 %collective-permute-done.2.l4 = bf16[128,384]{1,0:T(8,128)(2,1)S(1)} collective-permute-done((bf16[128,384]{1,0:T(8,128)(2,1)S(1)}, bf16[128,384]{1,0:T(8,128)(2,1)S(1)}, u32[]{:S(2)}, u32[]{:S(2)}) %collective-permute-start.2) | collective-permute-done | bytes 98336 | tf_op jit(solution)/shard_map/ppermute | solution.py:26
  44.2 0.0 copy-start.5
  44.2 1.5 %collective-permute-done.1.l2 = bf16[128,384]{1,0:T(8,128)(2,1)S(1)} collective-permute-done((bf16[128,384]{1,0:T(8,128)(2,1)S(1)}, bf16[128,384]{1,0:T(8,128)(2,1)S(1)}, u32[]{:S(2)}, u32[]{:S(2)}) %collective-permute-start.1) | collective-permute-done | bytes 98336 | tf_op jit(solution)/shard_map/ppermute | solution.py:26
  45.7 0.0 copy-start.6
  45.7 2.1 %collective-permute-done.l1 = bf16[128,384]{1,0:T(8,128)(2,1)S(1)} collective-permute-done((bf16[128,384]{1,0:T(8,128)(2,1)S(1)}, bf16[128,384]{1,0:T(8,128)(2,1)S(1)}, u32[]{:S(2)}, u32[]{:S(2)}) %collective-permute-start) | collective-permute-done | bytes 98336 | tf_op jit(solution)/shard_map/ppermute | solution.py:26
  47.7 0.0 copy-start.7
  47.7 0.0 all-to-all-done.got
  47.7 0.8 shard_map.104
  48.5 0.0 copy-done.5
  48.5 0.0 copy-done.6
  48.5 0.0 copy-done.7
  48.5 7.6 %all_to_all.15.got = bf16[8,32,256]{2,1,0:T(8,128)(2,1)S(1)} all-to-all(bf16[8,32,256]{2,1,0:T(8,128)(2,1)S(1)} %get-tuple-element.37), channel_id=1, replica_groups=mesh['z'=16,'x'=4,'core'=2,'head'=8] {'x','core'}, dimensions={0} | all-to-all | bytes 262144 | tf_op jit(solution)/shard_map/all_to_all | solution.py:35
  56.1 1.5 %shard_map.105 = bf16[8,128,384]{2,1,0:T(8,128)(2,1)} custom-call(bf16[8,32,256]{2,1,0:T(8,128)(2,1)S(1)} %all_to_all.15.got), custom_call_target="tpu_custom_call" | custom-call | flops 13000000 | bytes 917504 | tf_op jit(solution)/shard_map/pallas_call | solution.py:53
  57.6 0.0 copy-start.8
  57.6 6.9 %all-to-all-start.2 = ((bf16[8,128,384]{2,1,0:T(8,128)(2,1)}), bf16[8,128,384]{2,1,0:T(8,128)(2,1)S(1)}, u32[]{:S(2)}, u32[]{:S(2)}) async-start(bf16[8,128,384]{2,1,0:T(8,128)(2,1)} %shard_map.105), calls=%async_computation.2 | async-start | bytes 1572864 | tf_op jit(solution)/shard_map/all_to_all | solution.py:35
  64.5 0.0 copy-done.8
  64.5 0.0 copy-start
  64.5 3.7 %collective-permute-start.3 = (bf16[16,72,128]{2,1,0:T(8,128)(2,1)S(1)}, bf16[16,72,128]{2,1,0:T(8,128)(2,1)S(1)}, u32[]{:S(2)}, u32[]{:S(2)}) collective-permute-start(bf16[16,72,128]{2,1,0:T(8,128)(2,1)S(1)} %copy-done.8), channel_id=1, source_target_pairs={{0,16},{16,32},{32,48},{48,0},{1,17},{17,33},{33,49},{49,1},{2,18}... | collective-permute-start | bytes 884744 | tf_op jit(solution)/shard_map/ppermute | solution.py:31
  68.2 1.9 %collective-permute-start.5 = (bf16[16,72,128]{2,1,0:T(8,128)(2,1)S(1)}, bf16[16,72,128]{2,1,0:T(8,128)(2,1)S(1)}, u32[]{:S(2)}, u32[]{:S(2)}) collective-permute-start(bf16[16,72,128]{2,1,0:T(8,128)(2,1)S(1)} %copy-done.8), channel_id=1, source_target_pairs={{0,48},{16,0},{32,16},{48,32},{1,49},{17,1},{33,17},{49,33},{2,50}... | collective-permute-start | bytes 884744 | tf_op jit(solution)/shard_map/ppermute | solution.py:31
  70.2 3.7 %collective-permute-done.3.o1 = bf16[16,72,128]{2,1,0:T(8,128)(2,1)S(1)} collective-permute-done((bf16[16,72,128]{2,1,0:T(8,128)(2,1)S(1)}, bf16[16,72,128]{2,1,0:T(8,128)(2,1)S(1)}, u32[]{:S(2)}, u32[]{:S(2)}) %collective-permute-start.3) | collective-permute-done | bytes 294944 | tf_op jit(solution)/shard_map/ppermute | solution.py:31
  73.8 0.0 copy-start.9
  73.8 4.9 %collective-permute-start.4 = (bf16[16,72,128]{2,1,0:T(8,128)(2,1)S(1)}, bf16[16,72,128]{2,1,0:T(8,128)(2,1)S(1)}, u32[]{:S(2)}, u32[]{:S(2)}) collective-permute-start(bf16[16,72,128]{2,1,0:T(8,128)(2,1)S(1)} %collective-permute-done.3.o1), channel_id=1, source_target_pairs={{0,16},{16,32},{32,48},{48,0},{1,17},{17,33},{33,49},{49,1},{2,18}... | collective-permute-start | bytes 884744 | tf_op jit(solution)/shard_map/ppermute | solution.py:31
  78.8 1.9 %collective-permute-start.8 = (bf16[128,768]{1,0:T(8,128)(2,1)S(1)}, bf16[128,768]{1,0:T(8,128)(2,1)S(1)}, u32[]{:S(2)}, u32[]{:S(2)}) collective-permute-start(bf16[128,768]{1,0:T(8,128)(2,1)S(1)} %get-tuple-element.39), channel_id=1, source_target_pairs={{0,32},{8,40},{16,48},{24,56},{32,64},{40,72},{48,80},{56,88},{64,... | collective-permute-start | bytes 589832 | tf_op jit(solution)/shard_map/ppermute | solution.py:26
  80.7 3.4 %collective-permute-start.7 = (bf16[128,768]{1,0:T(8,128)(2,1)S(1)}, bf16[128,768]{1,0:T(8,128)(2,1)S(1)}, u32[]{:S(2)}, u32[]{:S(2)}) collective-permute-start(bf16[128,768]{1,0:T(8,128)(2,1)S(1)} %get-tuple-element.39), channel_id=1, source_target_pairs={{0,16},{8,24},{16,32},{24,40},{32,48},{40,56},{48,64},{56,72},{64,... | collective-permute-start | bytes 589832 | tf_op jit(solution)/shard_map/ppermute | solution.py:26
  84.1 7.0 %collective-permute-start.6 = (bf16[128,768]{1,0:T(8,128)(2,1)S(1)}, bf16[128,768]{1,0:T(8,128)(2,1)S(1)}, u32[]{:S(2)}, u32[]{:S(2)}) collective-permute-start(bf16[128,768]{1,0:T(8,128)(2,1)S(1)} %get-tuple-element.39), channel_id=1, source_target_pairs={{0,8},{8,16},{16,24},{24,32},{32,40},{40,48},{48,56},{56,64},{64,7... | collective-permute-start | bytes 589832 | tf_op jit(solution)/shard_map/ppermute | solution.py:26
  91.1 0.0 collective-permute-done.8.b4
  91.1 0.0 copy-start.1
  91.1 0.0 collective-permute-done.7.b2
  91.2 0.0 copy-start.2
  91.2 2.6 %collective-permute-done.6.b1 = bf16[128,768]{1,0:T(8,128)(2,1)S(1)} collective-permute-done((bf16[128,768]{1,0:T(8,128)(2,1)S(1)}, bf16[128,768]{1,0:T(8,128)(2,1)S(1)}, u32[]{:S(2)}, u32[]{:S(2)}) %collective-permute-start.6) | collective-permute-done | bytes 196640 | tf_op jit(solution)/shard_map/ppermute | solution.py:26
  93.7 0.0 copy-done.1
  93.7 0.0 copy-done.2
  93.7 0.0 copy-start.3
  93.7 0.7 copy-done.3
  94.4 0.0 copy-done
  94.4 3.6 %shard_map.106 = (f32[3,512,128]{2,1,0:T(8,128)}, f32[8,384]{1,0:T(8,128)}, f32[9,128,128]{2,1,0:T(8,128)}) custom-call(s32[1]{0:T(128)} %bitcast.frame, s32[1,2]{1,0:T(1,128)S(1)} %copy-done, bf16[128,384]{1,0:T(8,128)(2,1)} %query_h.3, bf16[128,384]{1,0:T(8,128)(2,1)} %key_h.5, bf16[128,384]{1,0:T(8,128)(2,1)} %value_h.5, bf16[128,768]{1,0:T(8,128)(2,1)} %copy-done.3, ...), custom_call_target="tpu_custom_call" | custom-call | flops 90000000 | bytes 2568204 | tf_op jit(solution)/shard_map/pallas_call | solution.py:53
  98.0 0.0 collective-permute-done.5.o3
  98.0 0.0 copy-start.10
  98.0 0.0 collective-permute-done.4.o2
  98.0 0.0 copy-start.11
  98.0 0.0 all-to-all-done.2.rows
  98.1 0.0 copy-done.9
  98.1 0.7 copy-done.10
  98.7 0.1 copy-done.11
  98.8 2.3 %shard_map.107 = (f32[128,384]{1,0:T(8,128)S(1)}, f32[128,384]{1,0:T(8,128)S(1)}, bf16[4,128,384]{2,1,0:T(8,128)(2,1)S(1)}, bf16[4,128,384]{2,1,0:T(8,128)(2,1)S...) custom-call(s32[1]{0:T(128)} %bitcast.frame, bf16[8,128,384]{2,1,0:T(8,128)(2,1)S(1)} %all-to-all-done.2.rows, ...), custom_call_target="tpu_custom_call" | custom-call | flops 350000000 | bytes 5529604 | tf_op jit(solution)/shard_map/pallas_call | solution.py:53
  101.1 2.1 %collective-permute-start.9 = (f32[128,384]{1,0:T(8,128)S(1)}, f32[128,384]{1,0:T(8,128)S(1)}, u32[]{:S(2)}, u32[]{:S(2)}) collective-permute-start(f32[128,384]{1,0:T(8,128)S(1)} %get-tuple-element.52), channel_id=1, source_target_pairs={{0,8},{8,0},{1,9},{9,1},{2,10},{10,2},{3,11},{11,3},{4,12},{12,4},... | collective-permute-start | bytes 589832 | tf_op jit(solution)/shard_map/ppermute | solution.py:31
  103.2 1.2 collective-permute-done.9.other
  104.4 0.9 shard_map.108
  105.4 6.9 %collective-permute-start.12 = (bf16[136,384]{1,0:T(8,128)(2,1)S(1)}, bf16[136,384]{1,0:T(8,128)(2,1)S(1)}, u32[]{:S(2)}, u32[]{:S(2)}) collective-permute-start(bf16[136,384]{1,0:T(8,128)(2,1)S(1)} %get-tuple-element.56.parcel), channel_id=1, source_target_pairs={{32,0},{40,8},{48,16},{56,24},{64,32},{72,40},{80,48},{88,56},{96,... | collective-permute-start | bytes 313352 | tf_op jit(solution)/shard_map/ppermute | solution.py:26
  112.3 1.9 %collective-permute-start.11 = (bf16[136,384]{1,0:T(8,128)(2,1)S(1)}, bf16[136,384]{1,0:T(8,128)(2,1)S(1)}, u32[]{:S(2)}, u32[]{:S(2)}) collective-permute-start(bf16[136,384]{1,0:T(8,128)(2,1)S(1)} %get-tuple-element.56.parcel), channel_id=1, source_target_pairs={{16,0},{24,8},{32,16},{40,24},{48,32},{56,40},{64,48},{72,56},{80,... | collective-permute-start | bytes 313352 | tf_op jit(solution)/shard_map/ppermute | solution.py:26
  114.2 2.6 %collective-permute-start.10 = (bf16[136,384]{1,0:T(8,128)(2,1)S(1)}, bf16[136,384]{1,0:T(8,128)(2,1)S(1)}, u32[]{:S(2)}, u32[]{:S(2)}) collective-permute-start(bf16[136,384]{1,0:T(8,128)(2,1)S(1)} %get-tuple-element.56.parcel), channel_id=1, source_target_pairs={{8,0},{16,8},{24,16},{32,24},{40,32},{48,40},{56,48},{64,56},{72,6... | collective-permute-start | bytes 313352 | tf_op jit(solution)/shard_map/ppermute | solution.py:26
  116.8 2.8 %shard_map.109 = (bf16[128,384]{1,0:T(8,128)(2,1)}, f32[128,384]{1,0:T(8,128)S(1)}, f32[128,384]{1,0:T(8,128)S(1)}, bf16[3,128,384]{2,1,0:T(8,128)(2,1)S(1)}, f32[9,128,128]{2,1,0:T(8,128)S(1)}) custom-call(bf16[136,384]{1,0:T(8,128)(2,1)S(1)} %get-tuple-element.56.parcel, f32[8,384]{1,0:T(8,128)S(1)} %get-tuple-element.57.row_dot, ...), custom_call_target="tpu_custom_call" | custom-call | flops 120000000 | bytes 4048896 | tf_op jit(solution)/shard_map/pallas_call | solution.py:53
  119.6 0.0 collective-permute-done.12.a4
  119.6 0.5 collective-permute-done.11.a2
  120.1 2.7 %collective-permute-done.10.a1 = bf16[136,384]{1,0:T(8,128)(2,1)S(1)} collective-permute-done((bf16[136,384]{1,0:T(8,128)(2,1)S(1)}, bf16[136,384]{1,0:T(8,128)(2,1)S(1)}, u32[]{:S(2)}, u32[]{:S(2)}) %collective-permute-start.10) | collective-permute-done | bytes 104480 | tf_op jit(solution)/shard_map/ppermute | solution.py:26
  122.9 1.3 %shard_map.110 = (bf16[128,384]{1,0:T(8,128)(2,1)}, bf16[128,384]{1,0:T(8,128)(2,1)}) custom-call(s32[1]{0:T(128)} %bitcast.frame, bf16[136,384]{1,0:T(8,128)(2,1)S(1)} %collective-permute-done.10.a1, bf16[136,384]{1,0:T(8,128)(2,1)S(1)} %collective-permute-done.11.a2, bf16[136,384]{1,0:T(8,128)(2,1)S(1)} %collective-permute-done.12.a4, ...), custom_call_target="tpu_custom_call" | custom-call | flops 120000000 | bytes 2181124 | tf_op jit(solution)/shard_map/pallas_call | solution.py:53
Async XLA Ops:
  2.6 18.8 %copy-start.4 = (bf16[128,384]{1,0:T(8,128)(2,1)S(1)}, bf16[128,384]{1,0:T(8,128)(2,1)}, u32[]{:S(2)}) copy-start(bf16[128,384]{1,0:T(8,128)(2,1)} %query_h.3) | copy-start | bytes 294916
  2.6 45.1 %all-to-all-start = ((bf16[16,104,128]{2,1,0:T(8,128)(2,1)}), bf16[16,104,128]{2,1,0:T(8,128)(2,1)S(1)}, u32[]{:S(2)}, u32[]{:S(2)}) async-start(bf16[16,104,128]{2,1,0:T(8,128)(2,1)} %get-tuple-element.35), calls=%async_computation | async-start | bytes 851968 | tf_op jit(solution)/shard_map/all_to_all | solution.py:35
  21.3 22.8 %collective-permute-start.2 = (bf16[128,384]{1,0:T(8,128)(2,1)S(1)}, bf16[128,384]{1,0:T(8,128)(2,1)S(1)}, u32[]{:S(2)}, u32[]{:S(2)}) collective-permute-start(bf16[128,384]{1,0:T(8,128)(2,1)S(1)} %copy-done.4), channel_id=1, source_target_pairs={{32,0},{40,8},{48,16},{56,24},{64,32},{72,40},{80,48},{88,56},{96,... | collective-permute-start | bytes 294920 | tf_op jit(solution)/shard_map/ppermute | solution.py:26
  24.4 21.3 %collective-permute-start.1 = (bf16[128,384]{1,0:T(8,128)(2,1)S(1)}, bf16[128,384]{1,0:T(8,128)(2,1)S(1)}, u32[]{:S(2)}, u32[]{:S(2)}) collective-permute-start(bf16[128,384]{1,0:T(8,128)(2,1)S(1)} %copy-done.4), channel_id=1, source_target_pairs={{16,0},{24,8},{32,16},{40,24},{48,32},{56,40},{64,48},{72,56},{80,... | collective-permute-start | bytes 294920 | tf_op jit(solution)/shard_map/ppermute | solution.py:26
  26.3 21.4 %collective-permute-start = (bf16[128,384]{1,0:T(8,128)(2,1)S(1)}, bf16[128,384]{1,0:T(8,128)(2,1)S(1)}, u32[]{:S(2)}, u32[]{:S(2)}) collective-permute-start(bf16[128,384]{1,0:T(8,128)(2,1)S(1)} %copy-done.4), channel_id=1, source_target_pairs={{8,0},{16,8},{24,16},{32,24},{40,32},{48,40},{56,48},{64,56},{72,6... | collective-permute-start | bytes 294920 | tf_op jit(solution)/shard_map/ppermute | solution.py:26
  44.2 4.3 %copy-start.5 = (bf16[128,384]{1,0:T(8,128)(2,1)}, bf16[128,384]{1,0:T(8,128)(2,1)S(1)}, u32[]{:S(2)}) copy-start(bf16[128,384]{1,0:T(8,128)(2,1)S(1)} %collective-permute-done.2.l4) | copy-start | bytes 294916
  45.7 2.8 %copy-start.6 = (bf16[128,384]{1,0:T(8,128)(2,1)}, bf16[128,384]{1,0:T(8,128)(2,1)S(1)}, u32[]{:S(2)}) copy-start(bf16[128,384]{1,0:T(8,128)(2,1)S(1)} %collective-permute-done.1.l2) | copy-start | bytes 294916
  47.7 0.8 copy-start.7
  57.6 7.0 %copy-start.8 = (bf16[16,72,128]{2,1,0:T(8,128)(2,1)S(1)}, bf16[16,72,128]{2,1,0:T(8,128)(2,1)}, u32[]{:S(2)}) copy-start(bf16[16,72,128]{2,1,0:T(8,128)(2,1)} %get-tuple-element.38.o0) | copy-start | bytes 884740
  57.6 40.5 %all-to-all-start.2 = ((bf16[8,128,384]{2,1,0:T(8,128)(2,1)}), bf16[8,128,384]{2,1,0:T(8,128)(2,1)S(1)}, u32[]{:S(2)}, u32[]{:S(2)}) async-start(bf16[8,128,384]{2,1,0:T(8,128)(2,1)} %shard_map.105), calls=%async_computation.2 | async-start | bytes 1572864 | tf_op jit(solution)/shard_map/all_to_all | solution.py:35
  64.5 29.9 %copy-start = (s32[1,2]{1,0:T(1,128)S(1)}, s32[1,2]{1,0:T(1,128)}, u32[]{:S(2)}) copy-start(s32[1,2]{1,0:T(1,128)} %band.3) | copy-start | bytes 28
  64.5 9.3 %collective-permute-start.3 = (bf16[16,72,128]{2,1,0:T(8,128)(2,1)S(1)}, bf16[16,72,128]{2,1,0:T(8,128)(2,1)S(1)}, u32[]{:S(2)}, u32[]{:S(2)}) collective-permute-start(bf16[16,72,128]{2,1,0:T(8,128)(2,1)S(1)} %copy-done.8), channel_id=1, source_target_pairs={{0,16},{16,32},{32,48},{48,0},{1,17},{17,33},{33,49},{49,1},{2,18}... | collective-permute-start | bytes 884744 | tf_op jit(solution)/shard_map/ppermute | solution.py:31
  68.2 29.8 %collective-permute-start.5 = (bf16[16,72,128]{2,1,0:T(8,128)(2,1)S(1)}, bf16[16,72,128]{2,1,0:T(8,128)(2,1)S(1)}, u32[]{:S(2)}, u32[]{:S(2)}) collective-permute-start(bf16[16,72,128]{2,1,0:T(8,128)(2,1)S(1)} %copy-done.8), channel_id=1, source_target_pairs={{0,48},{16,0},{32,16},{48,32},{1,49},{17,1},{33,17},{49,33},{2,50}... | collective-permute-start | bytes 884744 | tf_op jit(solution)/shard_map/ppermute | solution.py:31
  73.8 24.2 %copy-start.9 = (bf16[16,72,128]{2,1,0:T(8,128)(2,1)}, bf16[16,72,128]{2,1,0:T(8,128)(2,1)S(1)}, u32[]{:S(2)}) copy-start(bf16[16,72,128]{2,1,0:T(8,128)(2,1)S(1)} %collective-permute-done.3.o1) | copy-start | bytes 884740
  73.8 24.2 %collective-permute-start.4 = (bf16[16,72,128]{2,1,0:T(8,128)(2,1)S(1)}, bf16[16,72,128]{2,1,0:T(8,128)(2,1)S(1)}, u32[]{:S(2)}, u32[]{:S(2)}) collective-permute-start(bf16[16,72,128]{2,1,0:T(8,128)(2,1)S(1)} %collective-permute-done.3.o1), channel_id=1, source_target_pairs={{0,16},{16,32},{32,48},{48,0},{1,17},{17,33},{33,49},{49,1},{2,18}... | collective-permute-start | bytes 884744 | tf_op jit(solution)/shard_map/ppermute | solution.py:31
  78.8 12.4 %collective-permute-start.8 = (bf16[128,768]{1,0:T(8,128)(2,1)S(1)}, bf16[128,768]{1,0:T(8,128)(2,1)S(1)}, u32[]{:S(2)}, u32[]{:S(2)}) collective-permute-start(bf16[128,768]{1,0:T(8,128)(2,1)S(1)} %get-tuple-element.39), channel_id=1, source_target_pairs={{0,32},{8,40},{16,48},{24,56},{32,64},{40,72},{48,80},{56,88},{64,... | collective-permute-start | bytes 589832 | tf_op jit(solution)/shard_map/ppermute | solution.py:26
  80.7 10.5 %collective-permute-start.7 = (bf16[128,768]{1,0:T(8,128)(2,1)S(1)}, bf16[128,768]{1,0:T(8,128)(2,1)S(1)}, u32[]{:S(2)}, u32[]{:S(2)}) collective-permute-start(bf16[128,768]{1,0:T(8,128)(2,1)S(1)} %get-tuple-element.39), channel_id=1, source_target_pairs={{0,16},{8,24},{16,32},{24,40},{32,48},{40,56},{48,64},{56,72},{64,... | collective-permute-start | bytes 589832 | tf_op jit(solution)/shard_map/ppermute | solution.py:26
  84.1 9.6 %collective-permute-start.6 = (bf16[128,768]{1,0:T(8,128)(2,1)S(1)}, bf16[128,768]{1,0:T(8,128)(2,1)S(1)}, u32[]{:S(2)}, u32[]{:S(2)}) collective-permute-start(bf16[128,768]{1,0:T(8,128)(2,1)S(1)} %get-tuple-element.39), channel_id=1, source_target_pairs={{0,8},{8,16},{16,24},{24,32},{32,40},{40,48},{48,56},{56,64},{64,7... | collective-permute-start | bytes 589832 | tf_op jit(solution)/shard_map/ppermute | solution.py:26
  91.1 2.6 %copy-start.1 = (bf16[128,768]{1,0:T(8,128)(2,1)}, bf16[128,768]{1,0:T(8,128)(2,1)S(1)}, u32[]{:S(2)}) copy-start(bf16[128,768]{1,0:T(8,128)(2,1)S(1)} %collective-permute-done.8.b4) | copy-start | bytes 589828
  91.2 2.6 %copy-start.2 = (bf16[128,768]{1,0:T(8,128)(2,1)}, bf16[128,768]{1,0:T(8,128)(2,1)S(1)}, u32[]{:S(2)}) copy-start(bf16[128,768]{1,0:T(8,128)(2,1)S(1)} %collective-permute-done.7.b2) | copy-start | bytes 589828
  93.7 0.7 copy-start.3
  98.0 0.7 copy-start.10
  98.0 0.8 copy-start.11
  101.1 3.3 %collective-permute-start.9 = (f32[128,384]{1,0:T(8,128)S(1)}, f32[128,384]{1,0:T(8,128)S(1)}, u32[]{:S(2)}, u32[]{:S(2)}) collective-permute-start(f32[128,384]{1,0:T(8,128)S(1)} %get-tuple-element.52), channel_id=1, source_target_pairs={{0,8},{8,0},{1,9},{9,1},{2,10},{10,2},{3,11},{11,3},{4,12},{12,4},... | collective-permute-start | bytes 589832 | tf_op jit(solution)/shard_map/ppermute | solution.py:31
  105.4 14.2 %collective-permute-start.12 = (bf16[136,384]{1,0:T(8,128)(2,1)S(1)}, bf16[136,384]{1,0:T(8,128)(2,1)S(1)}, u32[]{:S(2)}, u32[]{:S(2)}) collective-permute-start(bf16[136,384]{1,0:T(8,128)(2,1)S(1)} %get-tuple-element.56.parcel), channel_id=1, source_target_pairs={{32,0},{40,8},{48,16},{56,24},{64,32},{72,40},{80,48},{88,56},{96,... | collective-permute-start | bytes 313352 | tf_op jit(solution)/shard_map/ppermute | solution.py:26
  112.3 7.8 %collective-permute-start.11 = (bf16[136,384]{1,0:T(8,128)(2,1)S(1)}, bf16[136,384]{1,0:T(8,128)(2,1)S(1)}, u32[]{:S(2)}, u32[]{:S(2)}) collective-permute-start(bf16[136,384]{1,0:T(8,128)(2,1)S(1)} %get-tuple-element.56.parcel), channel_id=1, source_target_pairs={{16,0},{24,8},{32,16},{40,24},{48,32},{56,40},{64,48},{72,56},{80,... | collective-permute-start | bytes 313352 | tf_op jit(solution)/shard_map/ppermute | solution.py:26
  114.2 8.6 %collective-permute-start.10 = (bf16[136,384]{1,0:T(8,128)(2,1)S(1)}, bf16[136,384]{1,0:T(8,128)(2,1)S(1)}, u32[]{:S(2)}, u32[]{:S(2)}) collective-permute-start(bf16[136,384]{1,0:T(8,128)(2,1)S(1)} %get-tuple-element.56.parcel), channel_id=1, source_target_pairs={{8,0},{16,8},{24,16},{32,24},{40,32},{48,40},{56,48},{64,56},{72,6... | collective-permute-start | bytes 313352 | tf_op jit(solution)/shard_map/ppermute | solution.py:26
where the time goes:
time: 125 us; the launch traced here: 124 us
  starting transfers between devices  70.1 us (56%)
  waiting for transfers between devices  29 us (23%)
  Pallas kernels  15 us (12%)
  blocking collectives  7.59 us (6%)
  local copies, waits for them, and re-layouts  1.48 us (1%)
    ppermute x9, starting transfers between devices, shifted(): return lax.ppermute(value, SEQ, pairs)  31.8 us
    all_to_all x2, starting transfers between devices, exchange(): return lax.all_to_all(value, axis, split_axis=0, concat_axis=0, tiled=True)  25.7 us
    ppermute x9, waiting for transfers between devices, shifted(): return lax.ppermute(value, SEQ, pairs)  24.1 us
    pallas_call x8, Pallas kernels, call(): pl.pallas_call(body, out_shape=[pltpu.HBM(s, t) if c == 'h' else jax.Shap...  15 us
    ppermute x4, starting transfers between devices, turned(): lax.ppermute(value, axis, [(i, (i + by) % peers) for i in range(peers)])  12.6 us
    all_to_all x1, blocking collectives, exchange(): return lax.all_to_all(value, axis, split_axis=0, concat_axis=0, tiled=True)  7.59 us
    ppermute x4, waiting for transfers between devices, turned(): lax.ppermute(value, axis, [(i, (i + by) % peers) for i in range(peers)])  4.89 us
  transfers between devices with their start and end apart: 15, of which 8 were waited for; matrix products, arithmetic and copies ran while one was open for 0% of the time, Pallas kernels for 5%

commit v1 on v0

--- a/solution.py
+++ b/solution.py
@@ -184,8 +184,8 @@
 
 
 def project_body(
-    frame, rows, o0, o1, o2, o3, key_h, value_h, b1, b2, b4, prob_h, norm_h,
-    mine, yours, keys, values, prob, norm, weight, sems
+    frame, rows, o0, o1, o2, o3, key_h, value_h, b1, b2, b4, prob_h, norm_h, query_h, l1, l2, l4, score_h,
+    mine, yours, keys, values, prob, norm, query, later, score, weight, sems
 ):
     x, core = (frame[0] >> 1) & 3, frame[0] & 1
     moves = []
@@ -196,6 +196,8 @@
     moves += [(key_h, keys.at[0]), (value_h, values.at[0]), (prob_h, prob), (norm_h, norm)]
     for i, pair in enumerate((b1, b2, b4)):
         moves += [(pair.at[:, :384], keys.at[i + 1]), (pair.at[:, 384:], values.at[i + 1])]
+    moves += [(query_h, query), (score_h, score)]
+    moves += [(b, later.at[i]) for i, b in enumerate((l1, l2, l4))]
     copies = started(moves, sems)
     wait(copies[:12])
     low = (iota((128, 128), 1) < 64).astype(F32).astype(BF16)
@@ -235,12 +237,8 @@
 
 
 def own_body(
-    parcel, row_dot, prob, query_h, keys, values, l1, l2, l4, score_h,
-    grad_query, key_part, value_part, later, score, query, sems
+    parcel, row_dot, prob, query, keys, values, grad_query, key_part, value_part
 ):
-    moves = [(query_h, query), (score_h, score)]
-    moves += [(b, later.at[i]) for i, b in enumerate((l1, l2, l4))]
-    copies = started(moves, sems)
     for h in range(3):
         g = parcel[:128, lanes(h)]
         total = None
@@ -251,12 +249,9 @@
             part = dot(s, keys[i, :, lanes(h)], 0, 0)
             total = part if total is None else total + part
             if i == 0:
-                if h == 0:
-                    wait(copies[:1])
                 key_part[:, lanes(h)] = dot(s, query[:, lanes(h)], 1, 0)
                 value_part[:, lanes(h)] = dot(p.astype(BF16), g, 1, 0)
         grad_query[:, lanes(h)] = (SCALE * total).astype(BF16)
-    wait(copies[1:])
 
 
 def later_body(frame, a1, a2, a4, later, score, values, key_part, value_part, grad_key, grad_value):
@@ -298,7 +293,7 @@
         pairs.append(shifted(pair, d))
     for d in DISTANCES[1:]:
         later.append(shifted(query_rows, -d))
-    got, *later = lax.optimization_barrier((got, *later))
+    got, later[0] = lax.optimization_barrier((got, later[0]))
     own, rows = call(split_body, [((16, 72, LANES), BF16), ((8, 32, 256), BF16)], "vhv", (got,), 70_000_000, (), 1)
     rows = exchange(rows, ("x", "core"))
     (rows,) = call(land_body, [((8, 128, 384), BF16)], "vv", (rows,), 13_000_000)
@@ -319,14 +314,16 @@
     )
     rows, far, left, prob, norm, score = lax.optimization_barrier((rows, far, left, prob, norm, score))
 
-    mine, yours, keys, values, prob, norm = call(
+    mine, yours, keys, values, prob, norm, query, later, score = call(
         project_body,
-        [((128, 384), F32)] * 2 + [((4, 128, 384), BF16)] * 2 + [((3, 512, 128), F32), ((8, 384), F32)],
-        "sv" + "h" * 11 + "v" * 6,
-        (frame, rows, own, right, far, left, key_rows, value_rows, *pairs, prob, norm),
+        [((128, 384), F32)] * 2
+        + [((4, 128, 384), BF16)] * 2
+        + [((3, 512, 128), F32), ((8, 384), F32), ((128, 384), BF16), ((3, 128, 384), BF16), ((9, 128, 128), F32)],
+        "sv" + "h" * 16 + "v" * 9,
+        (frame, rows, own, right, far, left, key_rows, value_rows, *pairs, prob, norm, query_rows, *later, score),
         350_000_000,
         [((16, 4, 24, 384), BF16)],
-        22,
+        27,
     )
     other = turned(yours, "core", 1)
     parcel, row_dot = call(
@@ -339,14 +336,12 @@
     boxes = []
     for d in DISTANCES[1:]:
         boxes.append(shifted(parcel, -d))
-    grad_query, key_part, value_part, later, score = call(
+    grad_query, key_part, value_part = call(
         own_body,
-        [((128, 384), BF16), ((128, 384), F32), ((128, 384), F32), ((3, 128, 384), BF16), ((9, 128, 128), F32)],
-        "vvvhvvhhhh" + "v" * 5,
-        (parcel, row_dot, prob, query_rows, keys, values, *later, score),
+        [((128, 384), BF16), ((128, 384), F32), ((128, 384), F32)],
+        "v" * 9,
+        (parcel, row_dot, prob, query, keys, values),
         120_000_000,
-        [((128, 384), BF16)],
-        5,
     )
     grad_key, grad_value = call(
         later_body,

time: 125 us -> 126 us (level)
  blocking collectives: 7.59 us -> 12.4 us
  starting transfers between devices: 70.1 us -> 68.2 us
  waiting for transfers between devices: 29 us -> 27.2 us
    all_to_all x1, blocking collectives: 7.59 us -> 12.4 us  [exchange(): return lax.all_to_all(value, axis, split_axis=0, concat_axis=0, tiled=True)]
    ppermute x4, waiting for transfers between devices: 4.89 us -> 1.06 us  [turned(): lax.ppermute(value, axis, [(i, (i + by) % peers) for i in range(peers)])]
    ppermute x9, starting transfers between devices: 31.8 us -> 28.5 us  [shifted(): return lax.ppermute(value, SEQ, pairs)]
    ppermute x9, waiting for transfers between devices: 24.1 us -> 26.2 us  [shifted(): return lax.ppermute(value, SEQ, pairs)]
    ppermute x4, starting transfers between devices: 12.6 us -> 14 us  [turned(): lax.ppermute(value, axis, [(i, (i + by) % peers) for i in range(peers)])]
  transfers between devices with their start and end apart: 15 -> 15, of which waited for: 8 -> 5; matrix products, arithmetic and copies ran while one was open for 0% -> 0% of each run, Pallas kernels for 5% -> 4%
where the time goes in v1:
time: 126 us; the launch traced here: 125 us
  starting transfers between devices  68.2 us (54%)
  waiting for transfers between devices  27.2 us (22%)
  Pallas kernels  14.3 us (11%)
  blocking collectives  12.4 us (10%)
  local copies, waits for them, and re-layouts  1.48 us (1%)
    ppermute x9, starting transfers between devices, shifted(): return lax.ppermute(value, SEQ, pairs)  28.5 us
    ppermute x9, waiting for transfers between devices, shifted(): return lax.ppermute(value, SEQ, pairs)  26.2 us
    all_to_all x2, starting transfers between devices, exchange(): return lax.all_to_all(value, axis, split_axis=0, concat_axis=0, tiled=True)  25.7 us
    pallas_call x8, Pallas kernels, call(): pl.pallas_call(body, out_shape=[pltpu.HBM(s, t) if c == 'h' else jax.Shap...  14.3 us
    ppermute x4, starting transfers between devices, turned(): lax.ppermute(value, axis, [(i, (i + by) % peers) for i in range(peers)])  14 us
    all_to_all x1, blocking collectives, exchange(): return lax.all_to_all(value, axis, split_axis=0, concat_axis=0, tiled=True)  12.4 us
  transfers between devices with their start and end apart: 15, of which 5 were waited for; matrix products, arithmetic and copies ran while one was open for 0% of the time, Pallas kernels for 4%

profile of v1, /device:TPU:7, one launch (start us, length us, event | category | flops | bytes accessed | tf_op | source)
XLA Modules:
  0.0 124.6 jit_solution(6229858992785281524)
XLA Ops:
  0.6 1.9 %shard_map.103 = (bf16[16,104,128]{2,1,0:T(8,128)(2,1)}, bf16[128,768]{1,0:T(8,128)(2,1)S(1)}) custom-call(s32[1]{0:T(128)} %bitcast.frame, s32[1,128]{1,0:T(1,128)} %bitcast.5, s32[1,128]{1,0:T(1,128)} %bitcast.6, bf16[128,384]{1,0:T(8,128)(2,1)} %grad_h.1, bf16[24,384]{1,0:T(8,128)(2,1)} %bitcast.4, bf16[128,384]{1,0:T(8,128)(2,1)} %key_h.5, ...), custom_call_target="tpu_custom_call" | custom-call | flops 13000000 | bytes 936964 | tf_op jit(solution)/shard_map/pallas_call | solution.py:53
  2.6 0.0 copy-start.4
  2.6 18.7 %all-to-all-start = ((bf16[16,104,128]{2,1,0:T(8,128)(2,1)}), bf16[16,104,128]{2,1,0:T(8,128)(2,1)S(1)}, u32[]{:S(2)}, u32[]{:S(2)}) async-start(bf16[16,104,128]{2,1,0:T(8,128)(2,1)} %get-tuple-element.34), calls=%async_computation | async-start | bytes 851968 | tf_op jit(solution)/shard_map/all_to_all | solution.py:35
  21.3 0.0 copy-done.4
  21.3 2.9 %collective-permute-start = (bf16[128,384]{1,0:T(8,128)(2,1)S(1)}, bf16[128,384]{1,0:T(8,128)(2,1)S(1)}, u32[]{:S(2)}, u32[]{:S(2)}) collective-permute-start(bf16[128,384]{1,0:T(8,128)(2,1)S(1)} %copy-done.4), channel_id=1, source_target_pairs={{8,0},{16,8},{24,16},{32,24},{40,32},{48,40},{56,48},{64,56},{72,6... | collective-permute-start | bytes 294920 | tf_op jit(solution)/shard_map/ppermute | solution.py:26
  24.2 18.6 %collective-permute-done.l1 = bf16[128,384]{1,0:T(8,128)(2,1)S(1)} collective-permute-done((bf16[128,384]{1,0:T(8,128)(2,1)S(1)}, bf16[128,384]{1,0:T(8,128)(2,1)S(1)}, u32[]{:S(2)}, u32[]{:S(2)}) %collective-permute-start) | collective-permute-done | bytes 98336 | tf_op jit(solution)/shard_map/ppermute | solution.py:26
  42.8 0.0 copy-start.5
  42.8 0.0 all-to-all-done.got
  42.8 0.8 shard_map.104
  43.5 0.0 copy-done.5
  43.6 12.4 %all_to_all.15.got = bf16[8,32,256]{2,1,0:T(8,128)(2,1)S(1)} all-to-all(bf16[8,32,256]{2,1,0:T(8,128)(2,1)S(1)} %get-tuple-element.36), channel_id=1, replica_groups=mesh['z'=16,'x'=4,'core'=2,'head'=8] {'x','core'}, dimensions={0} | all-to-all | bytes 262144 | tf_op jit(solution)/shard_map/all_to_all | solution.py:35
  55.9 1.5 %shard_map.105 = bf16[8,128,384]{2,1,0:T(8,128)(2,1)} custom-call(bf16[8,32,256]{2,1,0:T(8,128)(2,1)S(1)} %all_to_all.15.got), custom_call_target="tpu_custom_call" | custom-call | flops 13000000 | bytes 917504 | tf_op jit(solution)/shard_map/pallas_call | solution.py:53
  57.4 0.0 copy-start.8
  57.4 6.9 %all-to-all-start.2 = ((bf16[8,128,384]{2,1,0:T(8,128)(2,1)}), bf16[8,128,384]{2,1,0:T(8,128)(2,1)S(1)}, u32[]{:S(2)}, u32[]{:S(2)}) async-start(bf16[8,128,384]{2,1,0:T(8,128)(2,1)} %shard_map.105), calls=%async_computation.2 | async-start | bytes 1572864 | tf_op jit(solution)/shard_map/all_to_all | solution.py:35
  64.3 0.0 copy-done.8
  64.3 0.0 copy-start
  64.3 3.7 %collective-permute-start.1 = (bf16[16,72,128]{2,1,0:T(8,128)(2,1)S(1)}, bf16[16,72,128]{2,1,0:T(8,128)(2,1)S(1)}, u32[]{:S(2)}, u32[]{:S(2)}) collective-permute-start(bf16[16,72,128]{2,1,0:T(8,128)(2,1)S(1)} %copy-done.8), channel_id=1, source_target_pairs={{0,16},{16,32},{32,48},{48,0},{1,17},{17,33},{33,49},{49,1},{2,18}... | collective-permute-start | bytes 884744 | tf_op jit(solution)/shard_map/ppermute | solution.py:31
  68.0 2.1 %collective-permute-start.8 = (bf16[128,384]{1,0:T(8,128)(2,1)S(1)}, bf16[128,384]{1,0:T(8,128)(2,1)S(1)}, u32[]{:S(2)}, u32[]{:S(2)}) collective-permute-start(bf16[128,384]{1,0:T(8,128)(2,1)S(1)} %copy-done.4), channel_id=1, source_target_pairs={{32,0},{40,8},{48,16},{56,24},{64,32},{72,40},{80,48},{88,56},{96,... | collective-permute-start | bytes 294920 | tf_op jit(solution)/shard_map/ppermute | solution.py:26
  70.2 2.6 %collective-permute-start.7 = (bf16[128,384]{1,0:T(8,128)(2,1)S(1)}, bf16[128,384]{1,0:T(8,128)(2,1)S(1)}, u32[]{:S(2)}, u32[]{:S(2)}) collective-permute-start(bf16[128,384]{1,0:T(8,128)(2,1)S(1)} %copy-done.4), channel_id=1, source_target_pairs={{16,0},{24,8},{32,16},{40,24},{48,32},{56,40},{64,48},{72,56},{80,... | collective-permute-start | bytes 294920 | tf_op jit(solution)/shard_map/ppermute | solution.py:26
  72.7 1.9 %collective-permute-start.3 = (bf16[16,72,128]{2,1,0:T(8,128)(2,1)S(1)}, bf16[16,72,128]{2,1,0:T(8,128)(2,1)S(1)}, u32[]{:S(2)}, u32[]{:S(2)}) collective-permute-start(bf16[16,72,128]{2,1,0:T(8,128)(2,1)S(1)} %copy-done.8), channel_id=1, source_target_pairs={{0,48},{16,0},{32,16},{48,32},{1,49},{17,1},{33,17},{49,33},{2,50}... | collective-permute-start | bytes 884744 | tf_op jit(solution)/shard_map/ppermute | solution.py:31
  74.7 0.0 collective-permute-done.1.o1
  74.7 0.0 copy-start.9
  74.7 4.6 %collective-permute-start.2 = (bf16[16,72,128]{2,1,0:T(8,128)(2,1)S(1)}, bf16[16,72,128]{2,1,0:T(8,128)(2,1)S(1)}, u32[]{:S(2)}, u32[]{:S(2)}) collective-permute-start(bf16[16,72,128]{2,1,0:T(8,128)(2,1)S(1)} %collective-permute-done.1.o1), channel_id=1, source_target_pairs={{0,16},{16,32},{32,48},{48,0},{1,17},{17,33},{33,49},{49,1},{2,18}... | collective-permute-start | bytes 884744 | tf_op jit(solution)/shard_map/ppermute | solution.py:31
  79.3 4.0 %collective-permute-start.6 = (bf16[128,768]{1,0:T(8,128)(2,1)S(1)}, bf16[128,768]{1,0:T(8,128)(2,1)S(1)}, u32[]{:S(2)}, u32[]{:S(2)}) collective-permute-start(bf16[128,768]{1,0:T(8,128)(2,1)S(1)} %get-tuple-element.38), channel_id=1, source_target_pairs={{0,32},{8,40},{16,48},{24,56},{32,64},{40,72},{48,80},{56,88},{64,... | collective-permute-start | bytes 589832 | tf_op jit(solution)/shard_map/ppermute | solution.py:26
  83.3 0.0 collective-permute-done.8.l4
  83.3 0.0 copy-start.6
  83.3 3.7 %collective-permute-start.5 = (bf16[128,768]{1,0:T(8,128)(2,1)S(1)}, bf16[128,768]{1,0:T(8,128)(2,1)S(1)}, u32[]{:S(2)}, u32[]{:S(2)}) collective-permute-start(bf16[128,768]{1,0:T(8,128)(2,1)S(1)} %get-tuple-element.38), channel_id=1, source_target_pairs={{0,16},{8,24},{16,32},{24,40},{32,48},{40,56},{48,64},{56,72},{64,... | collective-permute-start | bytes 589832 | tf_op jit(solution)/shard_map/ppermute | solution.py:26
  87.0 0.0 collective-permute-done.7.l2
  87.0 0.0 copy-start.7
  87.0 4.6 %collective-permute-start.4 = (bf16[128,768]{1,0:T(8,128)(2,1)S(1)}, bf16[128,768]{1,0:T(8,128)(2,1)S(1)}, u32[]{:S(2)}, u32[]{:S(2)}) collective-permute-start(bf16[128,768]{1,0:T(8,128)(2,1)S(1)} %get-tuple-element.38), channel_id=1, source_target_pairs={{0,8},{8,16},{16,24},{24,32},{32,40},{40,48},{48,56},{56,64},{64,7... | collective-permute-start | bytes 589832 | tf_op jit(solution)/shard_map/ppermute | solution.py:26
  91.7 0.0 collective-permute-done.6.b4
  91.7 0.0 copy-start.1
  91.7 0.0 collective-permute-done.5.b2
  91.7 0.0 copy-start.2
  91.7 3.5 %collective-permute-done.4.b1 = bf16[128,768]{1,0:T(8,128)(2,1)S(1)} collective-permute-done((bf16[128,768]{1,0:T(8,128)(2,1)S(1)}, bf16[128,768]{1,0:T(8,128)(2,1)S(1)}, u32[]{:S(2)}, u32[]{:S(2)}) %collective-permute-start.4) | collective-permute-done | bytes 196640 | tf_op jit(solution)/shard_map/ppermute | solution.py:26
  95.2 0.0 copy-done.6
  95.2 0.0 copy-done.7
  95.2 0.0 copy-done.1
  95.2 0.0 copy-done.2
  95.2 0.0 copy-start.3
  95.2 0.7 copy-done.3
  95.9 0.0 copy-done
  95.9 3.6 %shard_map.106 = (f32[3,512,128]{2,1,0:T(8,128)}, f32[8,384]{1,0:T(8,128)}, f32[9,128,128]{2,1,0:T(8,128)}) custom-call(s32[1]{0:T(128)} %bitcast.frame, s32[1,2]{1,0:T(1,128)S(1)} %copy-done, bf16[128,384]{1,0:T(8,128)(2,1)} %query_h.3, bf16[128,384]{1,0:T(8,128)(2,1)} %key_h.5, bf16[128,384]{1,0:T(8,128)(2,1)} %value_h.5, bf16[128,768]{1,0:T(8,128)(2,1)} %copy-done.3, ...), custom_call_target="tpu_custom_call" | custom-call | flops 90000000 | bytes 2568204 | tf_op jit(solution)/shard_map/pallas_call | solution.py:53
  99.5 0.0 collective-permute-done.3.o3
  99.5 0.0 copy-start.10
  99.5 0.0 collective-permute-done.2.o2
  99.5 0.0 copy-start.11
  99.5 0.0 all-to-all-done.2.rows
  99.6 0.0 copy-done.9
  99.6 0.7 copy-done.10
  100.2 0.1 copy-done.11
  100.3 2.4 %shard_map.107 = (f32[128,384]{1,0:T(8,128)S(1)}, f32[128,384]{1,0:T(8,128)S(1)}, bf16[4,128,384]{2,1,0:T(8,128)(2,1)S(1)}, bf16[4,128,384]{2,1,0:T(8,128)(2,1)S...) custom-call(s32[1]{0:T(128)} %bitcast.frame, ...), custom_call_target="tpu_custom_call" | custom-call | flops 350000000 | bytes 7495684 | tf_op jit(solution)/shard_map/pallas_call | solution.py:53
  102.7 3.8 %collective-permute-start.9 = (f32[128,384]{1,0:T(8,128)S(1)}, f32[128,384]{1,0:T(8,128)S(1)}, u32[]{:S(2)}, u32[]{:S(2)}) collective-permute-start(f32[128,384]{1,0:T(8,128)S(1)} %get-tuple-element.50), channel_id=1, source_target_pairs={{0,8},{8,0},{1,9},{9,1},{2,10},{10,2},{3,11},{11,3},{4,12},{12,4},... | collective-permute-start | bytes 589832 | tf_op jit(solution)/shard_map/ppermute | solution.py:31
  106.5 1.0 collective-permute-done.9.other
  107.6 1.0 shard_map.108
  108.5 4.2 %collective-permute-start.12 = (bf16[136,384]{1,0:T(8,128)(2,1)S(1)}, bf16[136,384]{1,0:T(8,128)(2,1)S(1)}, u32[]{:S(2)}, u32[]{:S(2)}) collective-permute-start(bf16[136,384]{1,0:T(8,128)(2,1)S(1)} %get-tuple-element.54.parcel), channel_id=1, source_target_pairs={{32,0},{40,8},{48,16},{56,24},{64,32},{72,40},{80,48},{88,56},{96,... | collective-permute-start | bytes 313352 | tf_op jit(solution)/shard_map/ppermute | solution.py:26
  112.7 1.9 %collective-permute-start.11 = (bf16[136,384]{1,0:T(8,128)(2,1)S(1)}, bf16[136,384]{1,0:T(8,128)(2,1)S(1)}, u32[]{:S(2)}, u32[]{:S(2)}) collective-permute-start(bf16[136,384]{1,0:T(8,128)(2,1)S(1)} %get-tuple-element.54.parcel), channel_id=1, source_target_pairs={{16,0},{24,8},{32,16},{40,24},{48,32},{56,40},{64,48},{72,56},{80,... | collective-permute-start | bytes 313352 | tf_op jit(solution)/shard_map/ppermute | solution.py:26
  114.7 2.6 %collective-permute-start.10 = (bf16[136,384]{1,0:T(8,128)(2,1)S(1)}, bf16[136,384]{1,0:T(8,128)(2,1)S(1)}, u32[]{:S(2)}, u32[]{:S(2)}) collective-permute-start(bf16[136,384]{1,0:T(8,128)(2,1)S(1)} %get-tuple-element.54.parcel), channel_id=1, source_target_pairs={{8,0},{16,8},{24,16},{32,24},{40,32},{48,40},{56,48},{64,56},{72,6... | collective-permute-start | bytes 313352 | tf_op jit(solution)/shard_map/ppermute | solution.py:26
  117.2 2.0 %shard_map.109 = (bf16[128,384]{1,0:T(8,128)(2,1)}, f32[128,384]{1,0:T(8,128)S(1)}, f32[128,384]{1,0:T(8,128)S(1)}) custom-call(bf16[136,384]{1,0:T(8,128)(2,1)S(1)} %get-tuple-element.54.parcel, f32[8,384]{1,0:T(8,128)S(1)} %get-tuple-element.55.row_dot, f32[3,512,128]{2,1,0:T(8,128)S(1)} %get-tuple-element.52.prob, ...), custom_call_target="tpu_custom_call" | custom-call | flops 120000000 | bytes 2279424 | tf_op jit(solution)/shard_map/pallas_call | solution.py:53
  119.2 0.0 collective-permute-done.12.a4
  119.2 1.4 %collective-permute-done.11.a2 = bf16[136,384]{1,0:T(8,128)(2,1)S(1)} collective-permute-done((bf16[136,384]{1,0:T(8,128)(2,1)S(1)}, bf16[136,384]{1,0:T(8,128)(2,1)S(1)}, u32[]{:S(2)}, u32[]{:S(2)}) %collective-permute-start.11) | collective-permute-done | bytes 104480 | tf_op jit(solution)/shard_map/ppermute | solution.py:26
  120.6 2.7 %collective-permute-done.10.a1 = bf16[136,384]{1,0:T(8,128)(2,1)S(1)} collective-permute-done((bf16[136,384]{1,0:T(8,128)(2,1)S(1)}, bf16[136,384]{1,0:T(8,128)(2,1)S(1)}, u32[]{:S(2)}, u32[]{:S(2)}) %collective-permute-start.10) | collective-permute-done | bytes 104480 | tf_op jit(solution)/shard_map/ppermute | solution.py:26
  123.3 1.3 %shard_map.110 = (bf16[128,384]{1,0:T(8,128)(2,1)}, bf16[128,384]{1,0:T(8,128)(2,1)}) custom-call(s32[1]{0:T(128)} %bitcast.frame, bf16[136,384]{1,0:T(8,128)(2,1)S(1)} %collective-permute-done.10.a1, bf16[136,384]{1,0:T(8,128)(2,1)S(1)} %collective-permute-done.11.a2, bf16[136,384]{1,0:T(8,128)(2,1)S(1)} %collective-permute-done.12.a4, ...), custom_call_target="tpu_custom_call" | custom-call | flops 120000000 | bytes 2181124 | tf_op jit(solution)/shard_map/pallas_call | solution.py:53
Async XLA Ops:
  2.6 18.8 %copy-start.4 = (bf16[128,384]{1,0:T(8,128)(2,1)S(1)}, bf16[128,384]{1,0:T(8,128)(2,1)}, u32[]{:S(2)}) copy-start(bf16[128,384]{1,0:T(8,128)(2,1)} %query_h.3) | copy-start | bytes 294916
  2.6 40.2 %all-to-all-start = ((bf16[16,104,128]{2,1,0:T(8,128)(2,1)}), bf16[16,104,128]{2,1,0:T(8,128)(2,1)S(1)}, u32[]{:S(2)}, u32[]{:S(2)}) async-start(bf16[16,104,128]{2,1,0:T(8,128)(2,1)} %get-tuple-element.34), calls=%async_computation | async-start | bytes 851968 | tf_op jit(solution)/shard_map/all_to_all | solution.py:35
  21.3 21.4 %collective-permute-start = (bf16[128,384]{1,0:T(8,128)(2,1)S(1)}, bf16[128,384]{1,0:T(8,128)(2,1)S(1)}, u32[]{:S(2)}, u32[]{:S(2)}) collective-permute-start(bf16[128,384]{1,0:T(8,128)(2,1)S(1)} %copy-done.4), channel_id=1, source_target_pairs={{8,0},{16,8},{24,16},{32,24},{40,32},{48,40},{56,48},{64,56},{72,6... | collective-permute-start | bytes 294920 | tf_op jit(solution)/shard_map/ppermute | solution.py:26
  42.8 0.8 copy-start.5
  57.4 6.9 %copy-start.8 = (bf16[16,72,128]{2,1,0:T(8,128)(2,1)S(1)}, bf16[16,72,128]{2,1,0:T(8,128)(2,1)}, u32[]{:S(2)}) copy-start(bf16[16,72,128]{2,1,0:T(8,128)(2,1)} %get-tuple-element.37.o0) | copy-start | bytes 884740
  57.4 42.2 %all-to-all-start.2 = ((bf16[8,128,384]{2,1,0:T(8,128)(2,1)}), bf16[8,128,384]{2,1,0:T(8,128)(2,1)S(1)}, u32[]{:S(2)}, u32[]{:S(2)}) async-start(bf16[8,128,384]{2,1,0:T(8,128)(2,1)} %shard_map.105), calls=%async_computation.2 | async-start | bytes 1572864 | tf_op jit(solution)/shard_map/all_to_all | solution.py:35
  64.3 31.5 %copy-start = (s32[1,2]{1,0:T(1,128)S(1)}, s32[1,2]{1,0:T(1,128)}, u32[]{:S(2)}) copy-start(s32[1,2]{1,0:T(1,128)} %band.3) | copy-start | bytes 28
  64.3 10.3 %collective-permute-start.1 = (bf16[16,72,128]{2,1,0:T(8,128)(2,1)S(1)}, bf16[16,72,128]{2,1,0:T(8,128)(2,1)S(1)}, u32[]{:S(2)}, u32[]{:S(2)}) collective-permute-start(bf16[16,72,128]{2,1,0:T(8,128)(2,1)S(1)} %copy-done.8), channel_id=1, source_target_pairs={{0,16},{16,32},{32,48},{48,0},{1,17},{17,33},{33,49},{49,1},{2,18}... | collective-permute-start | bytes 884744 | tf_op jit(solution)/shard_map/ppermute | solution.py:31
  68.0 15.2 %collective-permute-start.8 = (bf16[128,384]{1,0:T(8,128)(2,1)S(1)}, bf16[128,384]{1,0:T(8,128)(2,1)S(1)}, u32[]{:S(2)}, u32[]{:S(2)}) collective-permute-start(bf16[128,384]{1,0:T(8,128)(2,1)S(1)} %copy-done.4), channel_id=1, source_target_pairs={{32,0},{40,8},{48,16},{56,24},{64,32},{72,40},{80,48},{88,56},{96,... | collective-permute-start | bytes 294920 | tf_op jit(solution)/shard_map/ppermute | solution.py:26
  70.2 16.8 %collective-permute-start.7 = (bf16[128,384]{1,0:T(8,128)(2,1)S(1)}, bf16[128,384]{1,0:T(8,128)(2,1)S(1)}, u32[]{:S(2)}, u32[]{:S(2)}) collective-permute-start(bf16[128,384]{1,0:T(8,128)(2,1)S(1)} %copy-done.4), channel_id=1, source_target_pairs={{16,0},{24,8},{32,16},{40,24},{48,32},{56,40},{64,48},{72,56},{80,... | collective-permute-start | bytes 294920 | tf_op jit(solution)/shard_map/ppermute | solution.py:26
  72.7 26.8 %collective-permute-start.3 = (bf16[16,72,128]{2,1,0:T(8,128)(2,1)S(1)}, bf16[16,72,128]{2,1,0:T(8,128)(2,1)S(1)}, u32[]{:S(2)}, u32[]{:S(2)}) collective-permute-start(bf16[16,72,128]{2,1,0:T(8,128)(2,1)S(1)} %copy-done.8), channel_id=1, source_target_pairs={{0,48},{16,0},{32,16},{48,32},{1,49},{17,1},{33,17},{49,33},{2,50}... | collective-permute-start | bytes 884744 | tf_op jit(solution)/shard_map/ppermute | solution.py:31
  74.7 24.9 %copy-start.9 = (bf16[16,72,128]{2,1,0:T(8,128)(2,1)}, bf16[16,72,128]{2,1,0:T(8,128)(2,1)S(1)}, u32[]{:S(2)}) copy-start(bf16[16,72,128]{2,1,0:T(8,128)(2,1)S(1)} %collective-permute-done.1.o1) | copy-start | bytes 884740
  74.7 24.8 %collective-permute-start.2 = (bf16[16,72,128]{2,1,0:T(8,128)(2,1)S(1)}, bf16[16,72,128]{2,1,0:T(8,128)(2,1)S(1)}, u32[]{:S(2)}, u32[]{:S(2)}) collective-permute-start(bf16[16,72,128]{2,1,0:T(8,128)(2,1)S(1)} %collective-permute-done.1.o1), channel_id=1, source_target_pairs={{0,16},{16,32},{32,48},{48,0},{1,17},{17,33},{33,49},{49,1},{2,18}... | collective-permute-start | bytes 884744 | tf_op jit(solution)/shard_map/ppermute | solution.py:31
  79.3 12.4 %collective-permute-start.6 = (bf16[128,768]{1,0:T(8,128)(2,1)S(1)}, bf16[128,768]{1,0:T(8,128)(2,1)S(1)}, u32[]{:S(2)}, u32[]{:S(2)}) collective-permute-start(bf16[128,768]{1,0:T(8,128)(2,1)S(1)} %get-tuple-element.38), channel_id=1, source_target_pairs={{0,32},{8,40},{16,48},{24,56},{32,64},{40,72},{48,80},{56,88},{64,... | collective-permute-start | bytes 589832 | tf_op jit(solution)/shard_map/ppermute | solution.py:26
  83.3 11.9 %copy-start.6 = (bf16[128,384]{1,0:T(8,128)(2,1)}, bf16[128,384]{1,0:T(8,128)(2,1)S(1)}, u32[]{:S(2)}) copy-start(bf16[128,384]{1,0:T(8,128)(2,1)S(1)} %collective-permute-done.8.l4) | copy-start | bytes 294916
  83.3 8.4 %collective-permute-start.5 = (bf16[128,768]{1,0:T(8,128)(2,1)S(1)}, bf16[128,768]{1,0:T(8,128)(2,1)S(1)}, u32[]{:S(2)}, u32[]{:S(2)}) collective-permute-start(bf16[128,768]{1,0:T(8,128)(2,1)S(1)} %get-tuple-element.38), channel_id=1, source_target_pairs={{0,16},{8,24},{16,32},{24,40},{32,48},{40,56},{48,64},{56,72},{64,... | collective-permute-start | bytes 589832 | tf_op jit(solution)/shard_map/ppermute | solution.py:26
  87.0 8.2 %copy-start.7 = (bf16[128,384]{1,0:T(8,128)(2,1)}, bf16[128,384]{1,0:T(8,128)(2,1)S(1)}, u32[]{:S(2)}) copy-start(bf16[128,384]{1,0:T(8,128)(2,1)S(1)} %collective-permute-done.7.l2) | copy-start | bytes 294916
  87.0 8.2 %collective-permute-start.4 = (bf16[128,768]{1,0:T(8,128)(2,1)S(1)}, bf16[128,768]{1,0:T(8,128)(2,1)S(1)}, u32[]{:S(2)}, u32[]{:S(2)}) collective-permute-start(bf16[128,768]{1,0:T(8,128)(2,1)S(1)} %get-tuple-element.38), channel_id=1, source_target_pairs={{0,8},{8,16},{16,24},{24,32},{32,40},{40,48},{48,56},{56,64},{64,7... | collective-permute-start | bytes 589832 | tf_op jit(solution)/shard_map/ppermute | solution.py:26
  91.7 3.5 %copy-start.1 = (bf16[128,768]{1,0:T(8,128)(2,1)}, bf16[128,768]{1,0:T(8,128)(2,1)S(1)}, u32[]{:S(2)}) copy-start(bf16[128,768]{1,0:T(8,128)(2,1)S(1)} %collective-permute-done.6.b4) | copy-start | bytes 589828
  91.7 3.5 %copy-start.2 = (bf16[128,768]{1,0:T(8,128)(2,1)}, bf16[128,768]{1,0:T(8,128)(2,1)S(1)}, u32[]{:S(2)}) copy-start(bf16[128,768]{1,0:T(8,128)(2,1)S(1)} %collective-permute-done.5.b2) | copy-start | bytes 589828
  95.2 0.7 copy-start.3
  99.5 0.7 copy-start.10
  99.5 0.8 copy-start.11
  102.7 4.9 %collective-permute-start.9 = (f32[128,384]{1,0:T(8,128)S(1)}, f32[128,384]{1,0:T(8,128)S(1)}, u32[]{:S(2)}, u32[]{:S(2)}) collective-permute-start(f32[128,384]{1,0:T(8,128)S(1)} %get-tuple-element.50), channel_id=1, source_target_pairs={{0,8},{8,0},{1,9},{9,1},{2,10},{10,2},{3,11},{11,3},{4,12},{12,4},... | collective-permute-start | bytes 589832 | tf_op jit(solution)/shard_map/ppermute | solution.py:31
  108.5 10.7 %collective-permute-start.12 = (bf16[136,384]{1,0:T(8,128)(2,1)S(1)}, bf16[136,384]{1,0:T(8,128)(2,1)S(1)}, u32[]{:S(2)}, u32[]{:S(2)}) collective-permute-start(bf16[136,384]{1,0:T(8,128)(2,1)S(1)} %get-tuple-element.54.parcel), channel_id=1, source_target_pairs={{32,0},{40,8},{48,16},{56,24},{64,32},{72,40},{80,48},{88,56},{96,... | collective-permute-start | bytes 313352 | tf_op jit(solution)/shard_map/ppermute | solution.py:26
  112.7 7.8 %collective-permute-start.11 = (bf16[136,384]{1,0:T(8,128)(2,1)S(1)}, bf16[136,384]{1,0:T(8,128)(2,1)S(1)}, u32[]{:S(2)}, u32[]{:S(2)}) collective-permute-start(bf16[136,384]{1,0:T(8,128)(2,1)S(1)} %get-tuple-element.54.parcel), channel_id=1, source_target_pairs={{16,0},{24,8},{32,16},{40,24},{48,32},{56,40},{64,48},{72,56},{80,... | collective-permute-start | bytes 313352 | tf_op jit(solution)/shard_map/ppermute | solution.py:26
  114.7 8.6 %collective-permute-start.10 = (bf16[136,384]{1,0:T(8,128)(2,1)S(1)}, bf16[136,384]{1,0:T(8,128)(2,1)S(1)}, u32[]{:S(2)}, u32[]{:S(2)}) collective-permute-start(bf16[136,384]{1,0:T(8,128)(2,1)S(1)} %get-tuple-element.54.parcel), channel_id=1, source_target_pairs={{8,0},{16,8},{24,16},{32,24},{40,32},{48,40},{56,48},{64,56},{72,6... | collective-permute-start | bytes 313352 | tf_op jit(solution)/shard_map/ppermute | solution.py:26

commit v2 on v1

--- a/solution.py
+++ b/solution.py
@@ -97,49 +97,36 @@
         piece = weight[:, lanes(h)]
         for z in range(16):
             out[z, 24 * h : 24 * h + 24, :] = piece
-            out[z, 72 + 8 * h : 80 + 8 * h, :] = rows[8 * z : 8 * z + 8, lanes(h)]
+            out[z, 80 + 8 * h : 88 + 8 * h, :] = rows[8 * z : 8 * z + 8, lanes(h)]
     for z in range(16):
-        out[z, 96:104, :] = where[8 * z : 8 * z + 8]
+        out[z, 72:80, :] = where[8 * z : 8 * z + 8]
     wait(copies[4:])
 
 
 def split_body(got, weight, rows, sems):
-    copies = started(((got.at[:, :72, :], weight),), sems)
+    copies = started(((got.at[:, :80, :], weight),), sems)
     row, col = iota((128, 128), 0), iota((128, 128), 1)
     order = (col == (row & 15) * 8 + (row >> 4)).astype(BF16)
     blocks = [
-        dot(order, got[:, 72 + 8 * b : 80 + 8 * b, :].reshape(128, LANES), 1, 0) for b in range(4)
+        dot(order, got[:, 80 + 8 * b : 88 + 8 * b, :].reshape(128, LANES), 1, 0) for b in range(3)
     ]
-    cell = iota((1, 512), 1)
-    at = cell & 255
-    source = ((at * 2731) >> 16) * 24 + at + (cell >> 8) * 24
-    source = jnp.where(at < 192, source, -1)
-    move = (iota((384, 512), 0) == source).astype(BF16)
-    sorted_rows = dot(jnp.concatenate(blocks[:3], axis=1).astype(BF16), move, 1, 0)
-    tag = jnp.where(iota((128, 256), 1) >= 192, jnp.concatenate([blocks[3]] * 2, axis=1), 0.0)
-    for core in range(2):
-        half = (sorted_rows[:, 256 * core : 256 * core + 256] + tag).astype(BF16)
-        for x in range(4):
-            rows[2 * x + core] = half[32 * x : 32 * x + 32]
+    cell = iota((1, 768), 1)
+    core = (cell >= 384).astype(jnp.int32)
+    at = cell - 384 * core
+    place = jnp.where(at < 192, at, jnp.where(at >= 320, at - 192, -1))
+    source = jnp.where(place >= 0, place + ((place * 2731) >> 16) * 24 + core * 24, -1)
+    move = (iota((384, 768), 0) == source).astype(BF16)
+    moved = dot(jnp.concatenate(blocks, axis=1).astype(BF16), move, 1, 0)
+    for x in range(4):
+        first, second = moved[32 * x : 32 * x + 16], moved[32 * x + 16 : 32 * x + 32]
+        for c in range(2):
+            begin = 3 * c
+            block = [first[:, lanes(begin)], second[:, lanes(begin)]]
+            block.append(first[:, lanes(begin + 1)] + second[:, lanes(begin + 2)])
+            block = jnp.concatenate(block, axis=0).astype(BF16)
+            for y in range(8):
+                rows[y, 2 * x + c] = block
     wait(copies)
-
-
-def land_body(got, out):
-    total = None
-    to = iota((1, 384), 1)
-    for c in range(2):
-        flat = got[:, 16 * c : 16 * c + 16, :].reshape(128, 256)
-        where = flat[:, 192:193].astype(F32) == iota((128, 128), 1).astype(F32)
-        rows = dot(where.astype(BF16), flat, 0, 0).astype(BF16)
-        first, second = to - 128 * c, to - 128 - 64 * c
-        source = jnp.where(
-            (first >= 0) & (first < 128), first, jnp.where((second >= 128) & (second < 192), second, -1)
-        )
-        part = dot(rows, (iota((256, 384), 0) == source).astype(BF16), 1, 0)
-        total = part if total is None else total + part
-    total = total.astype(BF16)
-    for y in range(8):
-        out[y] = total
 
 
 def forward_body(
@@ -185,7 +172,7 @@
 
 def project_body(
     frame, rows, o0, o1, o2, o3, key_h, value_h, b1, b2, b4, prob_h, norm_h, query_h, l1, l2, l4, score_h,
-    mine, yours, keys, values, prob, norm, query, later, score, weight, sems
+    mine, yours, keys, values, prob, norm, query, later, score, weight, places, sems
 ):
     x, core = (frame[0] >> 1) & 3, frame[0] & 1
     moves = []
@@ -193,33 +180,53 @@
         to_x = (x + 4 - turn) & 3
         for h in range(3):
             moves.append((piece.at[:, 24 * h : 24 * h + 24, :], weight.at[:, to_x, :, lanes(h)]))
+        moves.append((piece.at[:, 72:80, :], places.at[to_x]))
     moves += [(key_h, keys.at[0]), (value_h, values.at[0]), (prob_h, prob), (norm_h, norm)]
     for i, pair in enumerate((b1, b2, b4)):
         moves += [(pair.at[:, :384], keys.at[i + 1]), (pair.at[:, 384:], values.at[i + 1])]
     moves += [(query_h, query), (score_h, score)]
     moves += [(b, later.at[i]) for i, b in enumerate((l1, l2, l4))]
     copies = started(moves, sems)
-    wait(copies[:12])
+    wait(copies[:16])
     low = (iota((128, 128), 1) < 64).astype(F32).astype(BF16)
     high = (iota((128, 128), 1) >= 64).astype(F32).astype(BF16)
     total = None
     for y in range(8):
-        block = rows[y]
+        rest = rows[y, :, 32:48, :].reshape(128, LANES)
         both = [
-            jnp.concatenate([block[:, lanes(c)], block[:, 256:] * side], axis=1)
+            jnp.concatenate([rows[y, :, 16 * c : 16 * c + 16, :].reshape(128, LANES), rest * side], axis=1)
             for c, side in enumerate((low, high))
         ]
         block = weight[2 * y : 2 * y + 2].reshape(192, 384)
         block = jnp.concatenate([block, block[128:]], axis=0)
         part = dot(jnp.concatenate(both, axis=0), block, 1, 0)
         total = part if total is None else total + part
-    mine[...] = jnp.where(core == 0, total[:128], total[128:])
-    yours[...] = jnp.where(core == 0, total[128:], total[:128])
-    wait(copies[12:])
-
-
-def finish_body(band, mine, other, values, prob, norm, parcel, row_dot):
-    grad = (mine[...] + other[...]).astype(BF16)
+    where = places[...].astype(F32).reshape(64, 8, LANES)
+    for out, frame_core, half in (
+        (mine, core, jnp.where(core == 0, total[:128], total[128:])),
+        (yours, 1 - core, jnp.where(core == 0, total[128:], total[:128])),
+    ):
+        out[:128, :] = half
+        at = jnp.sum(jnp.where(iota((64, 8, LANES), 1) == 2 * x + frame_core, where, 0.0), axis=1)
+        tail = jnp.concatenate([at[48:], jnp.zeros((8, LANES), F32)], axis=0)
+        out[128:, :] = jnp.concatenate([at[:24], at[24:48], tail], axis=1)
+    wait(copies[16:])
+
+
+def places_of(half):
+    return jnp.concatenate([half[128:, lanes(0)], half[128:, lanes(1)], half[128:144, lanes(2)]], axis=0)
+
+
+def finish_body(frame, band, mine, other, values, prob, norm, parcel, row_dot):
+    core = frame[0] & 1
+    packed = (mine[:128, :] + other[:128, :]).astype(BF16)
+    own, far = places_of(mine), places_of(other)
+    first, second = jnp.where(core == 0, own, far), jnp.where(core == 0, far, own)
+    where = []
+    for x in range(4):
+        where += [first[16 * x : 16 * x + 16], second[16 * x : 16 * x + 16]]
+    where = jnp.concatenate(where, axis=0) == iota((128, 128), 1).astype(F32)
+    grad = dot(where.astype(F32).astype(BF16), packed, 0, 0).astype(BF16)
     parcel[:128, :] = grad
     dots = []
     for h in range(3):
@@ -294,10 +301,10 @@
     for d in DISTANCES[1:]:
         later.append(shifted(query_rows, -d))
     got, later[0] = lax.optimization_barrier((got, later[0]))
-    own, rows = call(split_body, [((16, 72, LANES), BF16), ((8, 32, 256), BF16)], "vhv", (got,), 70_000_000, (), 1)
-    rows = exchange(rows, ("x", "core"))
-    (rows,) = call(land_body, [((8, 128, 384), BF16)], "vv", (rows,), 13_000_000)
-    rows = exchange(rows, "head")
+    own, rows = call(
+        split_body, [((16, 80, LANES), BF16), ((8, 8, 48, LANES), BF16)], "vhv", (got,), 100_000_000, (), 1
+    )
+    rows = exchange(rows.reshape(64, 48, LANES), ("head", "x", "core")).reshape(8, 8, 48, LANES)
 
     right = turned(own, "x", 1)
     left = turned(own, "x", -1)
@@ -316,21 +323,21 @@
 
     mine, yours, keys, values, prob, norm, query, later, score = call(
         project_body,
-        [((128, 384), F32)] * 2
+        [((152, 384), F32)] * 2
         + [((4, 128, 384), BF16)] * 2
         + [((3, 512, 128), F32), ((8, 384), F32), ((128, 384), BF16), ((3, 128, 384), BF16), ((9, 128, 128), F32)],
         "sv" + "h" * 16 + "v" * 9,
         (frame, rows, own, right, far, left, key_rows, value_rows, *pairs, prob, norm, query_rows, *later, score),
         350_000_000,
-        [((16, 4, 24, 384), BF16)],
-        27,
+        [((16, 4, 24, 384), BF16), ((4, 16, 8, LANES), BF16)],
+        31,
     )
     other = turned(yours, "core", 1)
     parcel, row_dot = call(
         finish_body,
         [((136, 384), BF16), ((8, 384), F32)],
-        "s" + "v" * 7,
-        (band_widths, mine, other, values, prob, norm),
+        "ss" + "v" * 7,
+        (frame, band_widths, mine, other, values, prob, norm),
         50_000_000,
     )
     boxes = []

time: 126 us -> 131 us (1.040)
  blocking collectives: 12.4 us -> 0 us
  waiting for transfers between devices: 27.2 us -> 38.4 us
  starting transfers between devices: 68.2 us -> 74.4 us
    all_to_all x1 -> x0, blocking collectives: 12.4 us -> none  [exchange(): return lax.all_to_all(value, axis, split_axis=0, concat_axis=0, tiled=True)]
    ppermute x4, waiting for transfers between devices: 1.06 us -> 11.7 us  [turned(): lax.ppermute(value, axis, [(i, (i + by) % peers) for i in range(peers)])]
    all_to_all x2, starting transfers between devices: 25.7 us -> 33.7 us  [exchange(): return lax.all_to_all(value, axis, split_axis=0, concat_axis=0, tiled=True)]
    ppermute x4, starting transfers between devices: 14 us -> 12 us  [turned(): lax.ppermute(value, axis, [(i, (i + by) % peers) for i in range(peers)])]
    pallas_call x8 -> x7, Pallas kernels: 14.3 us -> 14.1 us  [call(): pl.pallas_call(body, out_shape=[pltpu.HBM(s, t) if c == 'h' else jax.Shap...]
  transfers between devices with their start and end apart: 15 -> 15, of which waited for: 5 -> 6; matrix products, arithmetic and copies ran while one was open for 0% -> 0% of each run, Pallas kernels for 4% -> 4%
where the time goes in v2:
time: 131 us; the launch traced here: 129 us
  starting transfers between devices  74.4 us (57%)
  waiting for transfers between devices  38.4 us (29%)
  Pallas kernels  14.1 us (11%)
  local copies, waits for them, and re-layouts  1.51 us (1%)
    all_to_all x2, starting transfers between devices, exchange(): return lax.all_to_all(value, axis, split_axis=0, concat_axis=0, tiled=True)  33.7 us
    ppermute x9, starting transfers between devices, shifted(): return lax.ppermute(value, SEQ, pairs)  28.7 us
    ppermute x9, waiting for transfers between devices, shifted(): return lax.ppermute(value, SEQ, pairs)  26.7 us
    pallas_call x7, Pallas kernels, call(): pl.pallas_call(body, out_shape=[pltpu.HBM(s, t) if c == 'h' else jax.Shap...  14.1 us
    ppermute x4, starting transfers between devices, turned(): lax.ppermute(value, axis, [(i, (i + by) % peers) for i in range(peers)])  12 us
    ppermute x4, waiting for transfers between devices, turned(): lax.ppermute(value, axis, [(i, (i + by) % peers) for i in range(peers)])  11.7 us
  transfers between devices with their start and end apart: 15, of which 6 were waited for; matrix products, arithmetic and copies ran while one was open for 0% of the time, Pallas kernels for 4%

profile of v2, /device:TPU:7, one launch (start us, length us, event | category | flops | bytes accessed | tf_op | source)
XLA Modules:
  0.0 129.4 jit_solution(8612996668446709178)
XLA Ops:
  0.6 1.9 %shard_map.103 = (bf16[16,104,128]{2,1,0:T(8,128)(2,1)}, bf16[128,768]{1,0:T(8,128)(2,1)S(1)}) custom-call(s32[1]{0:T(128)} %bitcast.frame, s32[1,128]{1,0:T(1,128)} %bitcast.8, s32[1,128]{1,0:T(1,128)} %bitcast.9, bf16[128,384]{1,0:T(8,128)(2,1)} %grad_h.1, bf16[24,384]{1,0:T(8,128)(2,1)} %bitcast.7, bf16[128,384]{1,0:T(8,128)(2,1)} %key_h.5, ...), custom_call_target="tpu_custom_call" | custom-call | flops 13000000 | bytes 936964 | tf_op jit(solution)/shard_map/pallas_call | solution.py:53
  2.6 0.0 copy-start.4
  2.6 18.7 %all-to-all-start = ((bf16[16,104,128]{2,1,0:T(8,128)(2,1)}), bf16[16,104,128]{2,1,0:T(8,128)(2,1)S(1)}, u32[]{:S(2)}, u32[]{:S(2)}) async-start(bf16[16,104,128]{2,1,0:T(8,128)(2,1)} %get-tuple-element.34), calls=%async_computation | async-start | bytes 851968 | tf_op jit(solution)/shard_map/all_to_all | solution.py:35
  21.3 0.0 copy-done.4
  21.3 2.9 %collective-permute-start = (bf16[128,384]{1,0:T(8,128)(2,1)S(1)}, bf16[128,384]{1,0:T(8,128)(2,1)S(1)}, u32[]{:S(2)}, u32[]{:S(2)}) collective-permute-start(bf16[128,384]{1,0:T(8,128)(2,1)S(1)} %copy-done.4), channel_id=1, source_target_pairs={{8,0},{16,8},{24,16},{32,24},{40,32},{48,40},{56,48},{64,56},{72,6... | collective-permute-start | bytes 294920 | tf_op jit(solution)/shard_map/ppermute | solution.py:26
  24.2 18.6 %collective-permute-done.l1 = bf16[128,384]{1,0:T(8,128)(2,1)S(1)} collective-permute-done((bf16[128,384]{1,0:T(8,128)(2,1)S(1)}, bf16[128,384]{1,0:T(8,128)(2,1)S(1)}, u32[]{:S(2)}, u32[]{:S(2)}) %collective-permute-start) | collective-permute-done | bytes 98336 | tf_op jit(solution)/shard_map/ppermute | solution.py:26
  42.8 0.0 copy-start.5
  42.8 0.0 all-to-all-done.got
  42.8 1.7 %shard_map.104 = (bf16[16,80,128]{2,1,0:T(8,128)(2,1)}, bf16[8,8,48,128]{3,2,1,0:T(8,128)(2,1)}) custom-call(bf16[16,104,128]{2,1,0:T(8,128)(2,1)S(1)} %all-to-all-done.got), custom_call_target="tpu_custom_call" | custom-call | flops 100000000 | bytes 1540096 | tf_op jit(solution)/shard_map/pallas_call | solution.py:53
  44.5 0.0 copy-done.5
  44.5 0.0 copy-start.8
  44.5 15.0 %all-to-all-start.1 = ((bf16[64,48,128]{2,1,0:T(8,128)(2,1)}), bf16[64,48,128]{2,1,0:T(8,128)(2,1)S(1)}, u32[]{:S(2)}, u32[]{:S(2)}) async-start(bf16[64,48,128]{2,1,0:T(8,128)(2,1)} %bitcast.4), calls=%async_computation.1 | async-start | bytes 1572864 | tf_op jit(solution)/shard_map/all_to_all | solution.py:35
  59.5 0.0 copy-done.8
  59.5 0.0 copy-start
  59.5 2.0 %collective-permute-start.1 = (bf16[16,80,128]{2,1,0:T(8,128)(2,1)S(1)}, bf16[16,80,128]{2,1,0:T(8,128)(2,1)S(1)}, u32[]{:S(2)}, u32[]{:S(2)}) collective-permute-start(bf16[16,80,128]{2,1,0:T(8,128)(2,1)S(1)} %copy-done.8), channel_id=1, source_target_pairs={{0,16},{16,32},{32,48},{48,0},{1,17},{17,33},{33,49},{49,1},{2,18}... | collective-permute-start | bytes 983048 | tf_op jit(solution)/shard_map/ppermute | solution.py:31
  61.5 3.3 %collective-permute-start.3 = (bf16[16,80,128]{2,1,0:T(8,128)(2,1)S(1)}, bf16[16,80,128]{2,1,0:T(8,128)(2,1)S(1)}, u32[]{:S(2)}, u32[]{:S(2)}) collective-permute-start(bf16[16,80,128]{2,1,0:T(8,128)(2,1)S(1)} %copy-done.8), channel_id=1, source_target_pairs={{0,48},{16,0},{32,16},{48,32},{1,49},{17,1},{33,17},{49,33},{2,50}... | collective-permute-start | bytes 983048 | tf_op jit(solution)/shard_map/ppermute | solution.py:31
  64.8 10.6 %collective-permute-done.1.o1 = bf16[16,80,128]{2,1,0:T(8,128)(2,1)S(1)} collective-permute-done((bf16[16,80,128]{2,1,0:T(8,128)(2,1)S(1)}, bf16[16,80,128]{2,1,0:T(8,128)(2,1)S(1)}, u32[]{:S(2)}, u32[]{:S(2)}) %collective-permute-start.1) | collective-permute-done | bytes 327712 | tf_op jit(solution)/shard_map/ppermute | solution.py:31
  75.4 0.0 copy-start.9
  75.4 3.4 %collective-permute-start.2 = (bf16[16,80,128]{2,1,0:T(8,128)(2,1)S(1)}, bf16[16,80,128]{2,1,0:T(8,128)(2,1)S(1)}, u32[]{:S(2)}, u32[]{:S(2)}) collective-permute-start(bf16[16,80,128]{2,1,0:T(8,128)(2,1)S(1)} %collective-permute-done.1.o1), channel_id=1, source_target_pairs={{0,16},{16,32},{32,48},{48,0},{1,17},{17,33},{33,49},{49,1},{2,18}... | collective-permute-start | bytes 983048 | tf_op jit(solution)/shard_map/ppermute | solution.py:31
  78.8 3.9 %collective-permute-start.8 = (bf16[128,384]{1,0:T(8,128)(2,1)S(1)}, bf16[128,384]{1,0:T(8,128)(2,1)S(1)}, u32[]{:S(2)}, u32[]{:S(2)}) collective-permute-start(bf16[128,384]{1,0:T(8,128)(2,1)S(1)} %copy-done.4), channel_id=1, source_target_pairs={{32,0},{40,8},{48,16},{56,24},{64,32},{72,40},{80,48},{88,56},{96,... | collective-permute-start | bytes 294920 | tf_op jit(solution)/shard_map/ppermute | solution.py:26
  82.7 1.9 %collective-permute-start.7 = (bf16[128,384]{1,0:T(8,128)(2,1)S(1)}, bf16[128,384]{1,0:T(8,128)(2,1)S(1)}, u32[]{:S(2)}, u32[]{:S(2)}) collective-permute-start(bf16[128,384]{1,0:T(8,128)(2,1)S(1)} %copy-done.4), channel_id=1, source_target_pairs={{16,0},{24,8},{32,16},{40,24},{48,32},{56,40},{64,48},{72,56},{80,... | collective-permute-start | bytes 294920 | tf_op jit(solution)/shard_map/ppermute | solution.py:26
  84.7 4.6 %collective-permute-start.6 = (bf16[128,768]{1,0:T(8,128)(2,1)S(1)}, bf16[128,768]{1,0:T(8,128)(2,1)S(1)}, u32[]{:S(2)}, u32[]{:S(2)}) collective-permute-start(bf16[128,768]{1,0:T(8,128)(2,1)S(1)} %get-tuple-element.38), channel_id=1, source_target_pairs={{0,32},{8,40},{16,48},{24,56},{32,64},{40,72},{48,80},{56,88},{64,... | collective-permute-start | bytes 589832 | tf_op jit(solution)/shard_map/ppermute | solution.py:26
  89.3 0.0 collective-permute-done.8.l4
  89.3 0.0 copy-start.6
  89.3 3.2 %collective-permute-start.5 = (bf16[128,768]{1,0:T(8,128)(2,1)S(1)}, bf16[128,768]{1,0:T(8,128)(2,1)S(1)}, u32[]{:S(2)}, u32[]{:S(2)}) collective-permute-start(bf16[128,768]{1,0:T(8,128)(2,1)S(1)} %get-tuple-element.38), channel_id=1, source_target_pairs={{0,16},{8,24},{16,32},{24,40},{32,48},{40,56},{48,64},{56,72},{64,... | collective-permute-start | bytes 589832 | tf_op jit(solution)/shard_map/ppermute | solution.py:26
  92.5 0.0 collective-permute-done.7.l2
  92.5 0.0 copy-start.7
  92.5 5.0 %collective-permute-start.4 = (bf16[128,768]{1,0:T(8,128)(2,1)S(1)}, bf16[128,768]{1,0:T(8,128)(2,1)S(1)}, u32[]{:S(2)}, u32[]{:S(2)}) collective-permute-start(bf16[128,768]{1,0:T(8,128)(2,1)S(1)} %get-tuple-element.38), channel_id=1, source_target_pairs={{0,8},{8,16},{16,24},{24,32},{32,40},{40,48},{48,56},{56,64},{64,7... | collective-permute-start | bytes 589832 | tf_op jit(solution)/shard_map/ppermute | solution.py:26
  97.5 0.0 collective-permute-done.6.b4
  97.5 0.0 copy-start.1
  97.5 0.0 collective-permute-done.5.b2
  97.5 0.0 copy-start.2
  97.5 4.0 %collective-permute-done.4.b1 = bf16[128,768]{1,0:T(8,128)(2,1)S(1)} collective-permute-done((bf16[128,768]{1,0:T(8,128)(2,1)S(1)}, bf16[128,768]{1,0:T(8,128)(2,1)S(1)}, u32[]{:S(2)}, u32[]{:S(2)}) %collective-permute-start.4) | collective-permute-done | bytes 196640 | tf_op jit(solution)/shard_map/ppermute | solution.py:26
  101.5 0.0 copy-done.6
  101.5 0.0 copy-done.7
  101.5 0.0 copy-done.1
  101.5 0.0 copy-done.2
  101.5 0.0 copy-start.3
  101.5 0.7 copy-done.3
  102.2 0.0 copy-done
  102.2 3.6 %shard_map.105 = (f32[3,512,128]{2,1,0:T(8,128)}, f32[8,384]{1,0:T(8,128)}, f32[9,128,128]{2,1,0:T(8,128)}) custom-call(s32[1]{0:T(128)} %bitcast.frame, s32[1,2]{1,0:T(1,128)S(1)} %copy-done, bf16[128,384]{1,0:T(8,128)(2,1)} %query_h.3, bf16[128,384]{1,0:T(8,128)(2,1)} %key_h.5, bf16[128,384]{1,0:T(8,128)(2,1)} %value_h.5, bf16[128,768]{1,0:T(8,128)(2,1)} %copy-done.3, ...), custom_call_target="tpu_custom_call" | custom-call | flops 90000000 | bytes 2568204 | tf_op jit(solution)/shard_map/pallas_call | solution.py:53
  105.8 0.0 collective-permute-done.3.o3
  105.8 0.0 copy-start.10
  105.8 0.0 collective-permute-done.2.o2
  105.8 0.0 copy-start.11
  105.8 0.0 all-to-all-done.1
  105.9 0.0 copy-done.9
  105.9 0.7 copy-done.10
  106.5 0.1 copy-done.11
  106.7 2.5 %shard_map.106 = (f32[152,384]{1,0:T(8,128)S(1)}, f32[152,384]{1,0:T(8,128)S(1)}, bf16[4,128,384]{2,1,0:T(8,128)(2,1)S(1)}, bf16[4,128,384]{2,1,0:T(8,128)(2,1)S...) custom-call(s32[1]{0:T(128)} %bitcast.frame, ...), custom_call_target="tpu_custom_call" | custom-call | flops 350000000 | bytes 7700484 | tf_op jit(solution)/shard_map/pallas_call | solution.py:53
  109.2 3.3 %collective-permute-start.9 = (f32[152,384]{1,0:T(8,128)S(1)}, f32[152,384]{1,0:T(8,128)S(1)}, u32[]{:S(2)}, u32[]{:S(2)}) collective-permute-start(f32[152,384]{1,0:T(8,128)S(1)} %get-tuple-element.50), channel_id=1, source_target_pairs={{0,8},{8,0},{1,9},{9,1},{2,10},{10,2},{3,11},{11,3},{4,12},{12,4},... | collective-permute-start | bytes 700424 | tf_op jit(solution)/shard_map/ppermute | solution.py:31
  112.5 1.1 collective-permute-done.9.other
  113.6 1.1 shard_map.107
  114.8 2.8 %collective-permute-start.12 = (bf16[136,384]{1,0:T(8,128)(2,1)S(1)}, bf16[136,384]{1,0:T(8,128)(2,1)S(1)}, u32[]{:S(2)}, u32[]{:S(2)}) collective-permute-start(bf16[136,384]{1,0:T(8,128)(2,1)S(1)} %get-tuple-element.54.parcel), channel_id=1, source_target_pairs={{32,0},{40,8},{48,16},{56,24},{64,32},{72,40},{80,48},{88,56},{96,... | collective-permute-start | bytes 313352 | tf_op jit(solution)/shard_map/ppermute | solution.py:26
  117.6 1.9 %collective-permute-start.11 = (bf16[136,384]{1,0:T(8,128)(2,1)S(1)}, bf16[136,384]{1,0:T(8,128)(2,1)S(1)}, u32[]{:S(2)}, u32[]{:S(2)}) collective-permute-start(bf16[136,384]{1,0:T(8,128)(2,1)S(1)} %get-tuple-element.54.parcel), channel_id=1, source_target_pairs={{16,0},{24,8},{32,16},{40,24},{48,32},{56,40},{64,48},{72,56},{80,... | collective-permute-start | bytes 313352 | tf_op jit(solution)/shard_map/ppermute | solution.py:26
  119.5 2.6 %collective-permute-start.10 = (bf16[136,384]{1,0:T(8,128)(2,1)S(1)}, bf16[136,384]{1,0:T(8,128)(2,1)S(1)}, u32[]{:S(2)}, u32[]{:S(2)}) collective-permute-start(bf16[136,384]{1,0:T(8,128)(2,1)S(1)} %get-tuple-element.54.parcel), channel_id=1, source_target_pairs={{8,0},{16,8},{24,16},{32,24},{40,32},{48,40},{56,48},{64,56},{72,6... | collective-permute-start | bytes 313352 | tf_op jit(solution)/shard_map/ppermute | solution.py:26
  122.1 2.0 %shard_map.108 = (bf16[128,384]{1,0:T(8,128)(2,1)}, f32[128,384]{1,0:T(8,128)S(1)}, f32[128,384]{1,0:T(8,128)S(1)}) custom-call(bf16[136,384]{1,0:T(8,128)(2,1)S(1)} %get-tuple-element.54.parcel, f32[8,384]{1,0:T(8,128)S(1)} %get-tuple-element.55.row_dot, f32[3,512,128]{2,1,0:T(8,128)S(1)} %get-tuple-element.52.prob, ...), custom_call_target="tpu_custom_call" | custom-call | flops 120000000 | bytes 2279424 | tf_op jit(solution)/shard_map/pallas_call | solution.py:53
  124.0 0.0 collective-permute-done.12.a4
  124.0 1.4 %collective-permute-done.11.a2 = bf16[136,384]{1,0:T(8,128)(2,1)S(1)} collective-permute-done((bf16[136,384]{1,0:T(8,128)(2,1)S(1)}, bf16[136,384]{1,0:T(8,128)(2,1)S(1)}, u32[]{:S(2)}, u32[]{:S(2)}) %collective-permute-start.11) | collective-permute-done | bytes 104480 | tf_op jit(solution)/shard_map/ppermute | solution.py:26
  125.4 2.7 %collective-permute-done.10.a1 = bf16[136,384]{1,0:T(8,128)(2,1)S(1)} collective-permute-done((bf16[136,384]{1,0:T(8,128)(2,1)S(1)}, bf16[136,384]{1,0:T(8,128)(2,1)S(1)}, u32[]{:S(2)}, u32[]{:S(2)}) %collective-permute-start.10) | collective-permute-done | bytes 104480 | tf_op jit(solution)/shard_map/ppermute | solution.py:26
  128.1 1.3 shard_map.109
Async XLA Ops:
  2.6 18.8 %copy-start.4 = (bf16[128,384]{1,0:T(8,128)(2,1)S(1)}, bf16[128,384]{1,0:T(8,128)(2,1)}, u32[]{:S(2)}) copy-start(bf16[128,384]{1,0:T(8,128)(2,1)} %query_h.3) | copy-start | bytes 294916
  2.6 40.2 %all-to-all-start = ((bf16[16,104,128]{2,1,0:T(8,128)(2,1)}), bf16[16,104,128]{2,1,0:T(8,128)(2,1)S(1)}, u32[]{:S(2)}, u32[]{:S(2)}) async-start(bf16[16,104,128]{2,1,0:T(8,128)(2,1)} %get-tuple-element.34), calls=%async_computation | async-start | bytes 851968 | tf_op jit(solution)/shard_map/all_to_all | solution.py:35
  21.3 21.4 %collective-permute-start = (bf16[128,384]{1,0:T(8,128)(2,1)S(1)}, bf16[128,384]{1,0:T(8,128)(2,1)S(1)}, u32[]{:S(2)}, u32[]{:S(2)}) collective-permute-start(bf16[128,384]{1,0:T(8,128)(2,1)S(1)} %copy-done.4), channel_id=1, source_target_pairs={{8,0},{16,8},{24,16},{32,24},{40,32},{48,40},{56,48},{64,56},{72,6... | collective-permute-start | bytes 294920 | tf_op jit(solution)/shard_map/ppermute | solution.py:26
  42.8 1.7 %copy-start.5 = (bf16[128,384]{1,0:T(8,128)(2,1)}, bf16[128,384]{1,0:T(8,128)(2,1)S(1)}, u32[]{:S(2)}) copy-start(bf16[128,384]{1,0:T(8,128)(2,1)S(1)} %collective-permute-done.l1) | copy-start | bytes 294916
  44.5 15.0 %copy-start.8 = (bf16[16,80,128]{2,1,0:T(8,128)(2,1)S(1)}, bf16[16,80,128]{2,1,0:T(8,128)(2,1)}, u32[]{:S(2)}) copy-start(bf16[16,80,128]{2,1,0:T(8,128)(2,1)} %get-tuple-element.37.o0) | copy-start | bytes 983044
  44.5 61.4 %all-to-all-start.1 = ((bf16[64,48,128]{2,1,0:T(8,128)(2,1)}), bf16[64,48,128]{2,1,0:T(8,128)(2,1)S(1)}, u32[]{:S(2)}, u32[]{:S(2)}) async-start(bf16[64,48,128]{2,1,0:T(8,128)(2,1)} %bitcast.4), calls=%async_computation.1 | async-start | bytes 1572864 | tf_op jit(solution)/shard_map/all_to_all | solution.py:35
  59.5 42.7 %copy-start = (s32[1,2]{1,0:T(1,128)S(1)}, s32[1,2]{1,0:T(1,128)}, u32[]{:S(2)}) copy-start(s32[1,2]{1,0:T(1,128)} %band.3) | copy-start | bytes 28
  59.5 15.9 %collective-permute-start.1 = (bf16[16,80,128]{2,1,0:T(8,128)(2,1)S(1)}, bf16[16,80,128]{2,1,0:T(8,128)(2,1)S(1)}, u32[]{:S(2)}, u32[]{:S(2)}) collective-permute-start(bf16[16,80,128]{2,1,0:T(8,128)(2,1)S(1)} %copy-done.8), channel_id=1, source_target_pairs={{0,16},{16,32},{32,48},{48,0},{1,17},{17,33},{33,49},{49,1},{2,18}... | collective-permute-start | bytes 983048 | tf_op jit(solution)/shard_map/ppermute | solution.py:31
  61.5 44.3 %collective-permute-start.3 = (bf16[16,80,128]{2,1,0:T(8,128)(2,1)S(1)}, bf16[16,80,128]{2,1,0:T(8,128)(2,1)S(1)}, u32[]{:S(2)}, u32[]{:S(2)}) collective-permute-start(bf16[16,80,128]{2,1,0:T(8,128)(2,1)S(1)} %copy-done.8), channel_id=1, source_target_pairs={{0,48},{16,0},{32,16},{48,32},{1,49},{17,1},{33,17},{49,33},{2,50}... | collective-permute-start | bytes 983048 | tf_op jit(solution)/shard_map/ppermute | solution.py:31
  75.4 30.5 %copy-start.9 = (bf16[16,80,128]{2,1,0:T(8,128)(2,1)}, bf16[16,80,128]{2,1,0:T(8,128)(2,1)S(1)}, u32[]{:S(2)}) copy-start(bf16[16,80,128]{2,1,0:T(8,128)(2,1)S(1)} %collective-permute-done.1.o1) | copy-start | bytes 983044
  75.4 30.4 %collective-permute-start.2 = (bf16[16,80,128]{2,1,0:T(8,128)(2,1)S(1)}, bf16[16,80,128]{2,1,0:T(8,128)(2,1)S(1)}, u32[]{:S(2)}, u32[]{:S(2)}) collective-permute-start(bf16[16,80,128]{2,1,0:T(8,128)(2,1)S(1)} %collective-permute-done.1.o1), channel_id=1, source_target_pairs={{0,16},{16,32},{32,48},{48,0},{1,17},{17,33},{33,49},{49,1},{2,18}... | collective-permute-start | bytes 983048 | tf_op jit(solution)/shard_map/ppermute | solution.py:31
  78.8 10.4 %collective-permute-start.8 = (bf16[128,384]{1,0:T(8,128)(2,1)S(1)}, bf16[128,384]{1,0:T(8,128)(2,1)S(1)}, u32[]{:S(2)}, u32[]{:S(2)}) collective-permute-start(bf16[128,384]{1,0:T(8,128)(2,1)S(1)} %copy-done.4), channel_id=1, source_target_pairs={{32,0},{40,8},{48,16},{56,24},{64,32},{72,40},{80,48},{88,56},{96,... | collective-permute-start | bytes 294920 | tf_op jit(solution)/shard_map/ppermute | solution.py:26
  82.7 9.7 %collective-permute-start.7 = (bf16[128,384]{1,0:T(8,128)(2,1)S(1)}, bf16[128,384]{1,0:T(8,128)(2,1)S(1)}, u32[]{:S(2)}, u32[]{:S(2)}) collective-permute-start(bf16[128,384]{1,0:T(8,128)(2,1)S(1)} %copy-done.4), channel_id=1, source_target_pairs={{16,0},{24,8},{32,16},{40,24},{48,32},{56,40},{64,48},{72,56},{80,... | collective-permute-start | bytes 294920 | tf_op jit(solution)/shard_map/ppermute | solution.py:26
  84.7 12.8 %collective-permute-start.6 = (bf16[128,768]{1,0:T(8,128)(2,1)S(1)}, bf16[128,768]{1,0:T(8,128)(2,1)S(1)}, u32[]{:S(2)}, u32[]{:S(2)}) collective-permute-start(bf16[128,768]{1,0:T(8,128)(2,1)S(1)} %get-tuple-element.38), channel_id=1, source_target_pairs={{0,32},{8,40},{16,48},{24,56},{32,64},{40,72},{48,80},{56,88},{64,... | collective-permute-start | bytes 589832 | tf_op jit(solution)/shard_map/ppermute | solution.py:26
  89.3 12.2 %copy-start.6 = (bf16[128,384]{1,0:T(8,128)(2,1)}, bf16[128,384]{1,0:T(8,128)(2,1)S(1)}, u32[]{:S(2)}) copy-start(bf16[128,384]{1,0:T(8,128)(2,1)S(1)} %collective-permute-done.8.l4) | copy-start | bytes 294916
  89.3 8.2 %collective-permute-start.5 = (bf16[128,768]{1,0:T(8,128)(2,1)S(1)}, bf16[128,768]{1,0:T(8,128)(2,1)S(1)}, u32[]{:S(2)}, u32[]{:S(2)}) collective-permute-start(bf16[128,768]{1,0:T(8,128)(2,1)S(1)} %get-tuple-element.38), channel_id=1, source_target_pairs={{0,16},{8,24},{16,32},{24,40},{32,48},{40,56},{48,64},{56,72},{64,... | collective-permute-start | bytes 589832 | tf_op jit(solution)/shard_map/ppermute | solution.py:26
  92.5 9.0 %copy-start.7 = (bf16[128,384]{1,0:T(8,128)(2,1)}, bf16[128,384]{1,0:T(8,128)(2,1)S(1)}, u32[]{:S(2)}) copy-start(bf16[128,384]{1,0:T(8,128)(2,1)S(1)} %collective-permute-done.7.l2) | copy-start | bytes 294916
  92.5 9.0 %collective-permute-start.4 = (bf16[128,768]{1,0:T(8,128)(2,1)S(1)}, bf16[128,768]{1,0:T(8,128)(2,1)S(1)}, u32[]{:S(2)}, u32[]{:S(2)}) collective-permute-start(bf16[128,768]{1,0:T(8,128)(2,1)S(1)} %get-tuple-element.38), channel_id=1, source_target_pairs={{0,8},{8,16},{16,24},{24,32},{32,40},{40,48},{48,56},{56,64},{64,7... | collective-permute-start | bytes 589832 | tf_op jit(solution)/shard_map/ppermute | solution.py:26
  97.5 4.0 %copy-start.1 = (bf16[128,768]{1,0:T(8,128)(2,1)}, bf16[128,768]{1,0:T(8,128)(2,1)S(1)}, u32[]{:S(2)}) copy-start(bf16[128,768]{1,0:T(8,128)(2,1)S(1)} %collective-permute-done.6.b4) | copy-start | bytes 589828
  97.5 4.0 %copy-start.2 = (bf16[128,768]{1,0:T(8,128)(2,1)}, bf16[128,768]{1,0:T(8,128)(2,1)S(1)}, u32[]{:S(2)}) copy-start(bf16[128,768]{1,0:T(8,128)(2,1)S(1)} %collective-permute-done.5.b2) | copy-start | bytes 589828
  101.5 0.7 copy-start.3
  105.8 0.7 copy-start.10
  105.8 0.8 copy-start.11
  109.2 4.4 %collective-permute-start.9 = (f32[152,384]{1,0:T(8,128)S(1)}, f32[152,384]{1,0:T(8,128)S(1)}, u32[]{:S(2)}, u32[]{:S(2)}) collective-permute-start(f32[152,384]{1,0:T(8,128)S(1)} %get-tuple-element.50), channel_id=1, source_target_pairs={{0,8},{8,0},{1,9},{9,1},{2,10},{10,2},{3,11},{11,3},{4,12},{12,4},... | collective-permute-start | bytes 700424 | tf_op jit(solution)/shard_map/ppermute | solution.py:31
  114.8 9.3 %collective-permute-start.12 = (bf16[136,384]{1,0:T(8,128)(2,1)S(1)}, bf16[136,384]{1,0:T(8,128)(2,1)S(1)}, u32[]{:S(2)}, u32[]{:S(2)}) collective-permute-start(bf16[136,384]{1,0:T(8,128)(2,1)S(1)} %get-tuple-element.54.parcel), channel_id=1, source_target_pairs={{32,0},{40,8},{48,16},{56,24},{64,32},{72,40},{80,48},{88,56},{96,... | collective-permute-start | bytes 313352 | tf_op jit(solution)/shard_map/ppermute | solution.py:26
  117.6 7.8 %collective-permute-start.11 = (bf16[136,384]{1,0:T(8,128)(2,1)S(1)}, bf16[136,384]{1,0:T(8,128)(2,1)S(1)}, u32[]{:S(2)}, u32[]{:S(2)}) collective-permute-start(bf16[136,384]{1,0:T(8,128)(2,1)S(1)} %get-tuple-element.54.parcel), channel_id=1, source_target_pairs={{16,0},{24,8},{32,16},{40,24},{48,32},{56,40},{64,48},{72,56},{80,... | collective-permute-start | bytes 313352 | tf_op jit(solution)/shard_map/ppermute | solution.py:26
  119.5 8.6 %collective-permute-start.10 = (bf16[136,384]{1,0:T(8,128)(2,1)S(1)}, bf16[136,384]{1,0:T(8,128)(2,1)S(1)}, u32[]{:S(2)}, u32[]{:S(2)}) collective-permute-start(bf16[136,384]{1,0:T(8,128)(2,1)S(1)} %get-tuple-element.54.parcel), channel_id=1, source_target_pairs={{8,0},{16,8},{24,16},{32,24},{40,32},{48,40},{56,48},{64,56},{72,6... | collective-permute-start | bytes 313352 | tf_op jit(solution)/shard_map/ppermute | solution.py:26

commit v3 on v2

--- a/solution.py
+++ b/solution.py
@@ -171,8 +171,8 @@
 
 
 def project_body(
-    frame, rows, o0, o1, o2, o3, key_h, value_h, b1, b2, b4, prob_h, norm_h, query_h, l1, l2, l4, score_h,
-    mine, yours, keys, values, prob, norm, query, later, score, weight, places, sems
+    frame, rows, o0, o1, o2, o3, key_h, value_h, b1, b2, b4, prob_h, norm_h,
+    mine, yours, keys, values, prob, norm, weight, places, sems
 ):
     x, core = (frame[0] >> 1) & 3, frame[0] & 1
     moves = []
@@ -184,8 +184,6 @@
     moves += [(key_h, keys.at[0]), (value_h, values.at[0]), (prob_h, prob), (norm_h, norm)]
     for i, pair in enumerate((b1, b2, b4)):
         moves += [(pair.at[:, :384], keys.at[i + 1]), (pair.at[:, 384:], values.at[i + 1])]
-    moves += [(query_h, query), (score_h, score)]
-    moves += [(b, later.at[i]) for i, b in enumerate((l1, l2, l4))]
     copies = started(moves, sems)
     wait(copies[:16])
     low = (iota((128, 128), 1) < 64).astype(F32).astype(BF16)
@@ -217,7 +215,13 @@
     return jnp.concatenate([half[128:, lanes(0)], half[128:, lanes(1)], half[128:144, lanes(2)]], axis=0)
 
 
-def finish_body(frame, band, mine, other, values, prob, norm, parcel, row_dot):
+def finish_body(
+    frame, band, mine, other, values, prob, norm, query_h, l1, l2, l4, score_h,
+    parcel, row_dot, query, later, score, sems
+):
+    moves = [(query_h, query), (score_h, score)]
+    moves += [(b, later.at[i]) for i, b in enumerate((l1, l2, l4))]
+    copies = started(moves, sems)
     core = frame[0] & 1
     packed = (mine[:128, :] + other[:128, :]).astype(BF16)
     own, far = places_of(mine), places_of(other)
@@ -241,6 +245,7 @@
     bands = [jnp.full((1, 384), band[0, i], jnp.int32).astype(F32) for i in range(2)]
     stack = [v.astype(F32) for v in parts_of(norm[:1]) + parts_of(dots)] + bands
     parcel[128:, :] = jnp.concatenate(stack, axis=0).astype(BF16)
+    wait(copies)
 
 
 def own_body(
@@ -300,7 +305,6 @@
         pairs.append(shifted(pair, d))
     for d in DISTANCES[1:]:
         later.append(shifted(query_rows, -d))
-    got, later[0] = lax.optimization_barrier((got, later[0]))
     own, rows = call(
         split_body, [((16, 80, LANES), BF16), ((8, 8, 48, LANES), BF16)], "vhv", (got,), 100_000_000, (), 1
     )
@@ -308,7 +312,7 @@
 
     right = turned(own, "x", 1)
     left = turned(own, "x", -1)
-    far = turned(right, "x", 1)
+    far = turned(left, "x", -1)
     prob, norm, score = call(
         forward_body,
         [((3, 512, 128), F32), ((8, 384), F32), ((9, 128, 128), F32)],
@@ -321,24 +325,24 @@
     )
     rows, far, left, prob, norm, score = lax.optimization_barrier((rows, far, left, prob, norm, score))
 
-    mine, yours, keys, values, prob, norm, query, later, score = call(
+    mine, yours, keys, values, prob, norm = call(
         project_body,
-        [((152, 384), F32)] * 2
-        + [((4, 128, 384), BF16)] * 2
-        + [((3, 512, 128), F32), ((8, 384), F32), ((128, 384), BF16), ((3, 128, 384), BF16), ((9, 128, 128), F32)],
-        "sv" + "h" * 16 + "v" * 9,
-        (frame, rows, own, right, far, left, key_rows, value_rows, *pairs, prob, norm, query_rows, *later, score),
+        [((152, 384), F32)] * 2 + [((4, 128, 384), BF16)] * 2 + [((3, 512, 128), F32), ((8, 384), F32)],
+        "svhv" + "h" * 9 + "v" * 6,
+        (frame, rows, own, right, far, left, key_rows, value_rows, *pairs, prob, norm),
         350_000_000,
         [((16, 4, 24, 384), BF16), ((4, 16, 8, LANES), BF16)],
-        31,
+        26,
     )
     other = turned(yours, "core", 1)
-    parcel, row_dot = call(
+    parcel, row_dot, query, later, score = call(
         finish_body,
-        [((136, 384), BF16), ((8, 384), F32)],
-        "ss" + "v" * 7,
-        (frame, band_widths, mine, other, values, prob, norm),
+        [((136, 384), BF16), ((8, 384), F32), ((128, 384), BF16), ((3, 128, 384), BF16), ((9, 128, 128), F32)],
+        "ss" + "v" * 5 + "h" * 5 + "v" * 5,
+        (frame, band_widths, mine, other, values, prob, norm, query_rows, *later, score),
         50_000_000,
+        (),
+        5,
     )
     boxes = []
     for d in DISTANCES[1:]:

time: 131 us -> 138 us (1.053)
  blocking collectives: 0 us -> 38.5 us
  starting transfers between devices: 74.4 us -> 54.9 us
  waiting for transfers between devices: 38.4 us -> 25.5 us
    all_to_all x0 -> x1, blocking collectives: none -> 38.5 us  [exchange(): return lax.all_to_all(value, axis, split_axis=0, concat_axis=0, tiled=True)]
    ppermute x9, waiting for transfers between devices: 26.7 us -> 8.68 us  [shifted(): return lax.ppermute(value, SEQ, pairs)]
    all_to_all x2 -> x1, starting transfers between devices: 33.7 us -> 16.3 us  [exchange(): return lax.all_to_all(value, axis, split_axis=0, concat_axis=0, tiled=True)]
    ppermute x4, waiting for transfers between devices: 11.7 us -> 16.8 us  [turned(): lax.ppermute(value, axis, [(i, (i + by) % peers) for i in range(peers)])]
    ppermute x9, starting transfers between devices: 28.7 us -> 26.9 us  [shifted(): return lax.ppermute(value, SEQ, pairs)]
  transfers between devices with their start and end apart: 15 -> 14, of which waited for: 6 -> 6; matrix products, arithmetic and copies ran while one was open for 0% -> 0% of each run, Pallas kernels for 4% -> 4%
where the time goes in v3:
time: 138 us; the launch traced here: 136 us
  starting transfers between devices  54.9 us (40%)
  blocking collectives  38.5 us (28%)
  waiting for transfers between devices  25.5 us (18%)
  Pallas kernels  14.3 us (10%)
  local copies, waits for them, and re-layouts  1.4 us (1%)
    all_to_all x1, blocking collectives, exchange(): return lax.all_to_all(value, axis, split_axis=0, concat_axis=0, tiled=True)  38.5 us
    ppermute x9, starting transfers between devices, shifted(): return lax.ppermute(value, SEQ, pairs)  26.9 us
    ppermute x4, waiting for transfers between devices, turned(): lax.ppermute(value, axis, [(i, (i + by) % peers) for i in range(peers)])  16.8 us
    all_to_all x1, starting transfers between devices, exchange(): return lax.all_to_all(value, axis, split_axis=0, concat_axis=0, tiled=True)  16.3 us
    pallas_call x7, Pallas kernels, call(): pl.pallas_call(body, out_shape=[pltpu.HBM(s, t) if c == 'h' else jax.Shap...  14.3 us
    ppermute x4, starting transfers between devices, turned(): lax.ppermute(value, axis, [(i, (i + by) % peers) for i in range(peers)])  11.7 us
    ppermute x9, waiting for transfers between devices, shifted(): return lax.ppermute(value, SEQ, pairs)  8.68 us
  transfers between devices with their start and end apart: 14, of which 6 were waited for; matrix products, arithmetic and copies ran while one was open for 0% of the time, Pallas kernels for 4%

profile of v3, /device:TPU:7, one launch (start us, length us, event | category | flops | bytes accessed | tf_op | source)
XLA Modules:
  0.0 135.6 jit_solution(10700296427750237675)
XLA Ops:
  0.6 1.2 shard_map.103
  1.8 38.5 %all_to_all.10.got = bf16[16,104,128]{2,1,0:T(8,128)(2,1)S(1)} all-to-all(bf16[16,104,128]{2,1,0:T(8,128)(2,1)S(1)} %get-tuple-element.32), channel_id=1, replica_groups=mesh['z'=16,'x'=4,'core'=2,'head'=8] {'z'}, dimensions={0} | all-to-all | bytes 851968 | tf_op jit(solution)/shard_map/all_to_all | solution.py:35
  40.4 1.6 %shard_map.104 = (bf16[16,80,128]{2,1,0:T(8,128)(2,1)}, bf16[8,8,48,128]{3,2,1,0:T(8,128)(2,1)}) custom-call(bf16[16,104,128]{2,1,0:T(8,128)(2,1)S(1)} %all_to_all.10.got), custom_call_target="tpu_custom_call" | custom-call | flops 100000000 | bytes 1540096 | tf_op jit(solution)/shard_map/pallas_call | solution.py:53
  42.0 0.0 copy-start.8
  42.0 0.0 copy-start.4
  42.0 16.3 %all-to-all-start.1 = ((bf16[64,48,128]{2,1,0:T(8,128)(2,1)}), bf16[64,48,128]{2,1,0:T(8,128)(2,1)S(1)}, u32[]{:S(2)}, u32[]{:S(2)}) async-start(bf16[64,48,128]{2,1,0:T(8,128)(2,1)} %bitcast.4), calls=%async_computation.1 | async-start | bytes 1572864 | tf_op jit(solution)/shard_map/all_to_all | solution.py:35
  58.3 0.0 copy-done.8
  58.3 0.0 copy-start
  58.4 2.5 %collective-permute-start = (bf16[16,80,128]{2,1,0:T(8,128)(2,1)S(1)}, bf16[16,80,128]{2,1,0:T(8,128)(2,1)S(1)}, u32[]{:S(2)}, u32[]{:S(2)}) collective-permute-start(bf16[16,80,128]{2,1,0:T(8,128)(2,1)S(1)} %copy-done.8), channel_id=1, source_target_pairs={{0,48},{16,0},{32,16},{48,32},{1,49},{17,1},{33,17},{49,33},{2,50}... | collective-permute-start | bytes 983048 | tf_op jit(solution)/shard_map/ppermute | solution.py:31
  60.8 15.7 %collective-permute-done.o3 = bf16[16,80,128]{2,1,0:T(8,128)(2,1)S(1)} collective-permute-done((bf16[16,80,128]{2,1,0:T(8,128)(2,1)S(1)}, bf16[16,80,128]{2,1,0:T(8,128)(2,1)S(1)}, u32[]{:S(2)}, u32[]{:S(2)}) %collective-permute-start) | collective-permute-done | bytes 327712 | tf_op jit(solution)/shard_map/ppermute | solution.py:31
  76.5 0.0 copy-start.9
  76.5 1.9 %collective-permute-start.1 = (bf16[16,80,128]{2,1,0:T(8,128)(2,1)S(1)}, bf16[16,80,128]{2,1,0:T(8,128)(2,1)S(1)}, u32[]{:S(2)}, u32[]{:S(2)}) collective-permute-start(bf16[16,80,128]{2,1,0:T(8,128)(2,1)S(1)} %collective-permute-done.o3), channel_id=1, source_target_pairs={{0,48},{16,0},{32,16},{48,32},{1,49},{17,1},{33,17},{49,33},{2,50}... | collective-permute-start | bytes 983048 | tf_op jit(solution)/shard_map/ppermute | solution.py:31
  78.5 4.6 %collective-permute-start.8 = (bf16[16,80,128]{2,1,0:T(8,128)(2,1)S(1)}, bf16[16,80,128]{2,1,0:T(8,128)(2,1)S(1)}, u32[]{:S(2)}, u32[]{:S(2)}) collective-permute-start(bf16[16,80,128]{2,1,0:T(8,128)(2,1)S(1)} %copy-done.8), channel_id=1, source_target_pairs={{0,16},{16,32},{32,48},{48,0},{1,17},{17,33},{33,49},{49,1},{2,18}... | collective-permute-start | bytes 983048 | tf_op jit(solution)/shard_map/ppermute | solution.py:31
  83.0 0.0 copy-done.4
  83.1 1.9 %collective-permute-start.7 = (bf16[128,384]{1,0:T(8,128)(2,1)S(1)}, bf16[128,384]{1,0:T(8,128)(2,1)S(1)}, u32[]{:S(2)}, u32[]{:S(2)}) collective-permute-start(bf16[128,384]{1,0:T(8,128)(2,1)S(1)} %copy-done.4), channel_id=1, source_target_pairs={{32,0},{40,8},{48,16},{56,24},{64,32},{72,40},{80,48},{88,56},{96,... | collective-permute-start | bytes 294920 | tf_op jit(solution)/shard_map/ppermute | solution.py:26
  85.0 2.5 %collective-permute-start.6 = (bf16[128,384]{1,0:T(8,128)(2,1)S(1)}, bf16[128,384]{1,0:T(8,128)(2,1)S(1)}, u32[]{:S(2)}, u32[]{:S(2)}) collective-permute-start(bf16[128,384]{1,0:T(8,128)(2,1)S(1)} %copy-done.4), channel_id=1, source_target_pairs={{16,0},{24,8},{32,16},{40,24},{48,32},{56,40},{64,48},{72,56},{80,... | collective-permute-start | bytes 294920 | tf_op jit(solution)/shard_map/ppermute | solution.py:26
  87.5 3.5 %collective-permute-start.5 = (bf16[128,384]{1,0:T(8,128)(2,1)S(1)}, bf16[128,384]{1,0:T(8,128)(2,1)S(1)}, u32[]{:S(2)}, u32[]{:S(2)}) collective-permute-start(bf16[128,384]{1,0:T(8,128)(2,1)S(1)} %copy-done.4), channel_id=1, source_target_pairs={{8,0},{16,8},{24,16},{32,24},{40,32},{48,40},{56,48},{64,56},{72,6... | collective-permute-start | bytes 294920 | tf_op jit(solution)/shard_map/ppermute | solution.py:26
  91.0 0.0 collective-permute-done.7.l4
  91.0 0.0 copy-start.5
  91.1 5.2 %collective-permute-start.4 = (bf16[128,768]{1,0:T(8,128)(2,1)S(1)}, bf16[128,768]{1,0:T(8,128)(2,1)S(1)}, u32[]{:S(2)}, u32[]{:S(2)}) collective-permute-start(bf16[128,768]{1,0:T(8,128)(2,1)S(1)} %get-tuple-element.35), channel_id=1, source_target_pairs={{0,32},{8,40},{16,48},{24,56},{32,64},{40,72},{48,80},{56,88},{64,... | collective-permute-start | bytes 589832 | tf_op jit(solution)/shard_map/ppermute | solution.py:26
  96.3 0.0 collective-permute-done.6.l2
  96.3 0.0 copy-start.6
  96.3 4.2 %collective-permute-start.3 = (bf16[128,768]{1,0:T(8,128)(2,1)S(1)}, bf16[128,768]{1,0:T(8,128)(2,1)S(1)}, u32[]{:S(2)}, u32[]{:S(2)}) collective-permute-start(bf16[128,768]{1,0:T(8,128)(2,1)S(1)} %get-tuple-element.35), channel_id=1, source_target_pairs={{0,16},{8,24},{16,32},{24,40},{32,48},{40,56},{48,64},{56,72},{64,... | collective-permute-start | bytes 589832 | tf_op jit(solution)/shard_map/ppermute | solution.py:26
  100.5 0.0 collective-permute-done.5.l1
  100.5 0.0 copy-start.7
  100.6 2.2 %collective-permute-start.2 = (bf16[128,768]{1,0:T(8,128)(2,1)S(1)}, bf16[128,768]{1,0:T(8,128)(2,1)S(1)}, u32[]{:S(2)}, u32[]{:S(2)}) collective-permute-start(bf16[128,768]{1,0:T(8,128)(2,1)S(1)} %get-tuple-element.35), channel_id=1, source_target_pairs={{0,8},{8,16},{16,24},{24,32},{32,40},{40,48},{48,56},{56,64},{64,7... | collective-permute-start | bytes 589832 | tf_op jit(solution)/shard_map/ppermute | solution.py:26
  102.8 0.0 collective-permute-done.4.b4
  102.8 0.0 copy-start.1
  102.8 1.7 %collective-permute-done.3.b2 = bf16[128,768]{1,0:T(8,128)(2,1)S(1)} collective-permute-done((bf16[128,768]{1,0:T(8,128)(2,1)S(1)}, bf16[128,768]{1,0:T(8,128)(2,1)S(1)}, u32[]{:S(2)}, u32[]{:S(2)}) %collective-permute-start.3) | collective-permute-done | bytes 196640 | tf_op jit(solution)/shard_map/ppermute | solution.py:26
  104.5 0.0 copy-start.2
  104.5 2.9 %collective-permute-done.2.b1 = bf16[128,768]{1,0:T(8,128)(2,1)S(1)} collective-permute-done((bf16[128,768]{1,0:T(8,128)(2,1)S(1)}, bf16[128,768]{1,0:T(8,128)(2,1)S(1)}, u32[]{:S(2)}, u32[]{:S(2)}) %collective-permute-start.2) | collective-permute-done | bytes 196640 | tf_op jit(solution)/shard_map/ppermute | solution.py:26
  107.3 0.0 copy-done.5
  107.3 0.0 copy-done.6
  107.4 0.0 copy-done.7
  107.4 0.0 copy-done.1
  107.4 0.0 copy-done.2
  107.4 0.0 copy-start.3
  107.4 0.7 copy-done.3
  108.0 0.0 copy-done
  108.0 3.6 %shard_map.105 = (f32[3,512,128]{2,1,0:T(8,128)}, f32[8,384]{1,0:T(8,128)}, f32[9,128,128]{2,1,0:T(8,128)}) custom-call(s32[1]{0:T(128)} %bitcast.frame, s32[1,2]{1,0:T(1,128)S(1)} %copy-done, bf16[128,384]{1,0:T(8,128)(2,1)} %query_h.3, bf16[128,384]{1,0:T(8,128)(2,1)} %key_h.5, bf16[128,384]{1,0:T(8,128)(2,1)} %value_h.5, bf16[128,768]{1,0:T(8,128)(2,1)} %copy-done.3, ...), custom_call_target="tpu_custom_call" | custom-call | flops 90000000 | bytes 2568204 | tf_op jit(solution)/shard_map/pallas_call | solution.py:53
  111.7 0.0 collective-permute-done.1.o2
  111.7 0.0 copy-start.10
  111.7 0.0 all-to-all-done.1
  111.7 0.0 collective-permute-done.8.o1
  111.7 0.0 copy-done.9
  111.7 0.7 copy-done.10
  112.4 2.4 %shard_map.106 = (f32[152,384]{1,0:T(8,128)S(1)}, f32[152,384]{1,0:T(8,128)S(1)}, bf16[4,128,384]{2,1,0:T(8,128)(2,1)S(1)}, bf16[4,128,384]{2,1,0:T(8,128)(2,1)S...) custom-call(s32[1]{0:T(128)} %bitcast.frame, bf16[8,8,48,128]{3,2,1,0:T(8,128)(2,1)S(1)} %bitcast.6, ...), custom_call_target="tpu_custom_call" | custom-call | flops 350000000 | bytes 5734404 | tf_op jit(solution)/shard_map/pallas_call | solution.py:53
  114.8 2.7 %collective-permute-start.9 = (f32[152,384]{1,0:T(8,128)S(1)}, f32[152,384]{1,0:T(8,128)S(1)}, u32[]{:S(2)}, u32[]{:S(2)}) collective-permute-start(f32[152,384]{1,0:T(8,128)S(1)} %get-tuple-element.45), channel_id=1, source_target_pairs={{0,8},{8,0},{1,9},{9,1},{2,10},{10,2},{3,11},{11,3},{4,12},{12,4},... | collective-permute-start | bytes 700424 | tf_op jit(solution)/shard_map/ppermute | solution.py:31
  117.5 1.1 collective-permute-done.9.other
  118.6 2.3 %shard_map.107 = (bf16[136,384]{1,0:T(8,128)(2,1)S(1)}, f32[8,384]{1,0:T(8,128)S(1)}, bf16[128,384]{1,0:T(8,128)(2,1)S(1)}, bf16[3,128,384]{2,1,0:T(8,128)(2,1)S(1)}, f32[9,128,128]{2,1,0:T(8,128)S(1)}) custom-call(s32[1]{0:T(128)} %bitcast.frame, s32[1,2]{1,0:T(1,128)S(1)} %copy-done, f32[152,384]{1,0:T(8,128)S(1)} %get-tuple-element.44.mine, ...), custom_call_target="tpu_custom_call" | custom-call | flops 50000000 | bytes 3741708 | tf_op jit(solution)/shard_map/pallas_call | solution.py:53
  120.9 2.8 %collective-permute-start.12 = (bf16[136,384]{1,0:T(8,128)(2,1)S(1)}, bf16[136,384]{1,0:T(8,128)(2,1)S(1)}, u32[]{:S(2)}, u32[]{:S(2)}) collective-permute-start(bf16[136,384]{1,0:T(8,128)(2,1)S(1)} %get-tuple-element.50.parcel), channel_id=1, source_target_pairs={{32,0},{40,8},{48,16},{56,24},{64,32},{72,40},{80,48},{88,56},{96,... | collective-permute-start | bytes 313352 | tf_op jit(solution)/shard_map/ppermute | solution.py:26
  123.7 1.9 %collective-permute-start.11 = (bf16[136,384]{1,0:T(8,128)(2,1)S(1)}, bf16[136,384]{1,0:T(8,128)(2,1)S(1)}, u32[]{:S(2)}, u32[]{:S(2)}) collective-permute-start(bf16[136,384]{1,0:T(8,128)(2,1)S(1)} %get-tuple-element.50.parcel), channel_id=1, source_target_pairs={{16,0},{24,8},{32,16},{40,24},{48,32},{56,40},{64,48},{72,56},{80,... | collective-permute-start | bytes 313352 | tf_op jit(solution)/shard_map/ppermute | solution.py:26
  125.6 2.6 %collective-permute-start.10 = (bf16[136,384]{1,0:T(8,128)(2,1)S(1)}, bf16[136,384]{1,0:T(8,128)(2,1)S(1)}, u32[]{:S(2)}, u32[]{:S(2)}) collective-permute-start(bf16[136,384]{1,0:T(8,128)(2,1)S(1)} %get-tuple-element.50.parcel), channel_id=1, source_target_pairs={{8,0},{16,8},{24,16},{32,24},{40,32},{48,40},{56,48},{64,56},{72,6... | collective-permute-start | bytes 313352 | tf_op jit(solution)/shard_map/ppermute | solution.py:26
  128.2 2.0 %shard_map.108 = (bf16[128,384]{1,0:T(8,128)(2,1)}, f32[128,384]{1,0:T(8,128)S(1)}, f32[128,384]{1,0:T(8,128)S(1)}) custom-call(bf16[136,384]{1,0:T(8,128)(2,1)S(1)} %get-tuple-element.50.parcel, f32[8,384]{1,0:T(8,128)S(1)} %get-tuple-element.51.row_dot, f32[3,512,128]{2,1,0:T(8,128)S(1)} %get-tuple-element.47.prob, ...), custom_call_target="tpu_custom_call" | custom-call | flops 120000000 | bytes 2279424 | tf_op jit(solution)/shard_map/pallas_call | solution.py:53
  130.2 0.0 collective-permute-done.12.a4
  130.2 1.1 collective-permute-done.11.a2
  131.2 3.0 %collective-permute-done.10.a1 = bf16[136,384]{1,0:T(8,128)(2,1)S(1)} collective-permute-done((bf16[136,384]{1,0:T(8,128)(2,1)S(1)}, bf16[136,384]{1,0:T(8,128)(2,1)S(1)}, u32[]{:S(2)}, u32[]{:S(2)}) %collective-permute-start.10) | collective-permute-done | bytes 104480 | tf_op jit(solution)/shard_map/ppermute | solution.py:26
  134.3 1.3 shard_map.109
Async XLA Ops:
  42.0 16.3 %copy-start.8 = (bf16[16,80,128]{2,1,0:T(8,128)(2,1)S(1)}, bf16[16,80,128]{2,1,0:T(8,128)(2,1)}, u32[]{:S(2)}) copy-start(bf16[16,80,128]{2,1,0:T(8,128)(2,1)} %get-tuple-element.34.o0) | copy-start | bytes 983044
  42.0 41.0 %copy-start.4 = (bf16[128,384]{1,0:T(8,128)(2,1)S(1)}, bf16[128,384]{1,0:T(8,128)(2,1)}, u32[]{:S(2)}) copy-start(bf16[128,384]{1,0:T(8,128)(2,1)} %query_h.3) | copy-start | bytes 294916
  42.0 69.7 %all-to-all-start.1 = ((bf16[64,48,128]{2,1,0:T(8,128)(2,1)}), bf16[64,48,128]{2,1,0:T(8,128)(2,1)S(1)}, u32[]{:S(2)}, u32[]{:S(2)}) async-start(bf16[64,48,128]{2,1,0:T(8,128)(2,1)} %bitcast.4), calls=%async_computation.1 | async-start | bytes 1572864 | tf_op jit(solution)/shard_map/all_to_all | solution.py:35
  58.3 49.7 %copy-start = (s32[1,2]{1,0:T(1,128)S(1)}, s32[1,2]{1,0:T(1,128)}, u32[]{:S(2)}) copy-start(s32[1,2]{1,0:T(1,128)} %band.3) | copy-start | bytes 28
  58.4 18.2 %collective-permute-start = (bf16[16,80,128]{2,1,0:T(8,128)(2,1)S(1)}, bf16[16,80,128]{2,1,0:T(8,128)(2,1)S(1)}, u32[]{:S(2)}, u32[]{:S(2)}) collective-permute-start(bf16[16,80,128]{2,1,0:T(8,128)(2,1)S(1)} %copy-done.8), channel_id=1, source_target_pairs={{0,48},{16,0},{32,16},{48,32},{1,49},{17,1},{33,17},{49,33},{2,50}... | collective-permute-start | bytes 983048 | tf_op jit(solution)/shard_map/ppermute | solution.py:31
  76.5 35.2 %copy-start.9 = (bf16[16,80,128]{2,1,0:T(8,128)(2,1)}, bf16[16,80,128]{2,1,0:T(8,128)(2,1)S(1)}, u32[]{:S(2)}) copy-start(bf16[16,80,128]{2,1,0:T(8,128)(2,1)S(1)} %collective-permute-done.o3) | copy-start | bytes 983044
  76.5 35.1 %collective-permute-start.1 = (bf16[16,80,128]{2,1,0:T(8,128)(2,1)S(1)}, bf16[16,80,128]{2,1,0:T(8,128)(2,1)S(1)}, u32[]{:S(2)}, u32[]{:S(2)}) collective-permute-start(bf16[16,80,128]{2,1,0:T(8,128)(2,1)S(1)} %collective-permute-done.o3), channel_id=1, source_target_pairs={{0,48},{16,0},{32,16},{48,32},{1,49},{17,1},{33,17},{49,33},{2,50}... | collective-permute-start | bytes 983048 | tf_op jit(solution)/shard_map/ppermute | solution.py:31
  78.5 33.2 %collective-permute-start.8 = (bf16[16,80,128]{2,1,0:T(8,128)(2,1)S(1)}, bf16[16,80,128]{2,1,0:T(8,128)(2,1)S(1)}, u32[]{:S(2)}, u32[]{:S(2)}) collective-permute-start(bf16[16,80,128]{2,1,0:T(8,128)(2,1)S(1)} %copy-done.8), channel_id=1, source_target_pairs={{0,16},{16,32},{32,48},{48,0},{1,17},{17,33},{33,49},{49,1},{2,18}... | collective-permute-start | bytes 983048 | tf_op jit(solution)/shard_map/ppermute | solution.py:31
  83.1 8.0 %collective-permute-start.7 = (bf16[128,384]{1,0:T(8,128)(2,1)S(1)}, bf16[128,384]{1,0:T(8,128)(2,1)S(1)}, u32[]{:S(2)}, u32[]{:S(2)}) collective-permute-start(bf16[128,384]{1,0:T(8,128)(2,1)S(1)} %copy-done.4), channel_id=1, source_target_pairs={{32,0},{40,8},{48,16},{56,24},{64,32},{72,40},{80,48},{88,56},{96,... | collective-permute-start | bytes 294920 | tf_op jit(solution)/shard_map/ppermute | solution.py:26
  85.0 11.3 %collective-permute-start.6 = (bf16[128,384]{1,0:T(8,128)(2,1)S(1)}, bf16[128,384]{1,0:T(8,128)(2,1)S(1)}, u32[]{:S(2)}, u32[]{:S(2)}) collective-permute-start(bf16[128,384]{1,0:T(8,128)(2,1)S(1)} %copy-done.4), channel_id=1, source_target_pairs={{16,0},{24,8},{32,16},{40,24},{48,32},{56,40},{64,48},{72,56},{80,... | collective-permute-start | bytes 294920 | tf_op jit(solution)/shard_map/ppermute | solution.py:26
  87.5 13.1 %collective-permute-start.5 = (bf16[128,384]{1,0:T(8,128)(2,1)S(1)}, bf16[128,384]{1,0:T(8,128)(2,1)S(1)}, u32[]{:S(2)}, u32[]{:S(2)}) collective-permute-start(bf16[128,384]{1,0:T(8,128)(2,1)S(1)} %copy-done.4), channel_id=1, source_target_pairs={{8,0},{16,8},{24,16},{32,24},{40,32},{48,40},{56,48},{64,56},{72,6... | collective-permute-start | bytes 294920 | tf_op jit(solution)/shard_map/ppermute | solution.py:26
  91.0 16.3 %copy-start.5 = (bf16[128,384]{1,0:T(8,128)(2,1)}, bf16[128,384]{1,0:T(8,128)(2,1)S(1)}, u32[]{:S(2)}) copy-start(bf16[128,384]{1,0:T(8,128)(2,1)S(1)} %collective-permute-done.7.l4) | copy-start | bytes 294916
  91.1 11.7 %collective-permute-start.4 = (bf16[128,768]{1,0:T(8,128)(2,1)S(1)}, bf16[128,768]{1,0:T(8,128)(2,1)S(1)}, u32[]{:S(2)}, u32[]{:S(2)}) collective-permute-start(bf16[128,768]{1,0:T(8,128)(2,1)S(1)} %get-tuple-element.35), channel_id=1, source_target_pairs={{0,32},{8,40},{16,48},{24,56},{32,64},{40,72},{48,80},{56,88},{64,... | collective-permute-start | bytes 589832 | tf_op jit(solution)/shard_map/ppermute | solution.py:26
  96.3 11.1 %copy-start.6 = (bf16[128,384]{1,0:T(8,128)(2,1)}, bf16[128,384]{1,0:T(8,128)(2,1)S(1)}, u32[]{:S(2)}) copy-start(bf16[128,384]{1,0:T(8,128)(2,1)S(1)} %collective-permute-done.6.l2) | copy-start | bytes 294916
  96.3 8.2 %collective-permute-start.3 = (bf16[128,768]{1,0:T(8,128)(2,1)S(1)}, bf16[128,768]{1,0:T(8,128)(2,1)S(1)}, u32[]{:S(2)}, u32[]{:S(2)}) collective-permute-start(bf16[128,768]{1,0:T(8,128)(2,1)S(1)} %get-tuple-element.35), channel_id=1, source_target_pairs={{0,16},{8,24},{16,32},{24,40},{32,48},{40,56},{48,64},{56,72},{64,... | collective-permute-start | bytes 589832 | tf_op jit(solution)/shard_map/ppermute | solution.py:26
  100.5 6.8 %copy-start.7 = (bf16[128,384]{1,0:T(8,128)(2,1)}, bf16[128,384]{1,0:T(8,128)(2,1)S(1)}, u32[]{:S(2)}) copy-start(bf16[128,384]{1,0:T(8,128)(2,1)S(1)} %collective-permute-done.5.l1) | copy-start | bytes 294916
  100.6 6.8 %collective-permute-start.2 = (bf16[128,768]{1,0:T(8,128)(2,1)S(1)}, bf16[128,768]{1,0:T(8,128)(2,1)S(1)}, u32[]{:S(2)}, u32[]{:S(2)}) collective-permute-start(bf16[128,768]{1,0:T(8,128)(2,1)S(1)} %get-tuple-element.35), channel_id=1, source_target_pairs={{0,8},{8,16},{16,24},{24,32},{32,40},{40,48},{48,56},{56,64},{64,7... | collective-permute-start | bytes 589832 | tf_op jit(solution)/shard_map/ppermute | solution.py:26
  102.8 4.6 %copy-start.1 = (bf16[128,768]{1,0:T(8,128)(2,1)}, bf16[128,768]{1,0:T(8,128)(2,1)S(1)}, u32[]{:S(2)}) copy-start(bf16[128,768]{1,0:T(8,128)(2,1)S(1)} %collective-permute-done.4.b4) | copy-start | bytes 589828
  104.5 2.9 %copy-start.2 = (bf16[128,768]{1,0:T(8,128)(2,1)}, bf16[128,768]{1,0:T(8,128)(2,1)S(1)}, u32[]{:S(2)}) copy-start(bf16[128,768]{1,0:T(8,128)(2,1)S(1)} %collective-permute-done.3.b2) | copy-start | bytes 589828
  107.4 0.7 copy-start.3
  111.7 0.7 copy-start.10
  114.8 3.8 %collective-permute-start.9 = (f32[152,384]{1,0:T(8,128)S(1)}, f32[152,384]{1,0:T(8,128)S(1)}, u32[]{:S(2)}, u32[]{:S(2)}) collective-permute-start(f32[152,384]{1,0:T(8,128)S(1)} %get-tuple-element.45), channel_id=1, source_target_pairs={{0,8},{8,0},{1,9},{9,1},{2,10},{10,2},{3,11},{11,3},{4,12},{12,4},... | collective-permute-start | bytes 700424 | tf_op jit(solution)/shard_map/ppermute | solution.py:31
  120.9 9.3 %collective-permute-start.12 = (bf16[136,384]{1,0:T(8,128)(2,1)S(1)}, bf16[136,384]{1,0:T(8,128)(2,1)S(1)}, u32[]{:S(2)}, u32[]{:S(2)}) collective-permute-start(bf16[136,384]{1,0:T(8,128)(2,1)S(1)} %get-tuple-element.50.parcel), channel_id=1, source_target_pairs={{32,0},{40,8},{48,16},{56,24},{64,32},{72,40},{80,48},{88,56},{96,... | collective-permute-start | bytes 313352 | tf_op jit(solution)/shard_map/ppermute | solution.py:26
  123.7 7.5 %collective-permute-start.11 = (bf16[136,384]{1,0:T(8,128)(2,1)S(1)}, bf16[136,384]{1,0:T(8,128)(2,1)S(1)}, u32[]{:S(2)}, u32[]{:S(2)}) collective-permute-start(bf16[136,384]{1,0:T(8,128)(2,1)S(1)} %get-tuple-element.50.parcel), channel_id=1, source_target_pairs={{16,0},{24,8},{32,16},{40,24},{48,32},{56,40},{64,48},{72,56},{80,... | collective-permute-start | bytes 313352 | tf_op jit(solution)/shard_map/ppermute | solution.py:26
  125.6 8.7 %collective-permute-start.10 = (bf16[136,384]{1,0:T(8,128)(2,1)S(1)}, bf16[136,384]{1,0:T(8,128)(2,1)S(1)}, u32[]{:S(2)}, u32[]{:S(2)}) collective-permute-start(bf16[136,384]{1,0:T(8,128)(2,1)S(1)} %get-tuple-element.50.parcel), channel_id=1, source_target_pairs={{8,0},{16,8},{24,16},{32,24},{40,32},{48,40},{56,48},{64,56},{72,6... | collective-permute-start | bytes 313352 | tf_op jit(solution)/shard_map/ppermute | solution.py:26

commit v4 on v2

--- a/solution.py
+++ b/solution.py
@@ -300,7 +300,6 @@
         pairs.append(shifted(pair, d))
     for d in DISTANCES[1:]:
         later.append(shifted(query_rows, -d))
-    got, later[0] = lax.optimization_barrier((got, later[0]))
     own, rows = call(
         split_body, [((16, 80, LANES), BF16), ((8, 8, 48, LANES), BF16)], "vhv", (got,), 100_000_000, (), 1
     )
@@ -308,7 +307,7 @@
 
     right = turned(own, "x", 1)
     left = turned(own, "x", -1)
-    far = turned(right, "x", 1)
+    far = turned(left, "x", -1)
     prob, norm, score = call(
         forward_body,
         [((3, 512, 128), F32), ((8, 384), F32), ((9, 128, 128), F32)],
@@ -326,7 +325,7 @@
         [((152, 384), F32)] * 2
         + [((4, 128, 384), BF16)] * 2
         + [((3, 512, 128), F32), ((8, 384), F32), ((128, 384), BF16), ((3, 128, 384), BF16), ((9, 128, 128), F32)],
-        "sv" + "h" * 16 + "v" * 9,
+        "svhv" + "h" * 14 + "v" * 9,
         (frame, rows, own, right, far, left, key_rows, value_rows, *pairs, prob, norm, query_rows, *later, score),
         350_000_000,
         [((16, 4, 24, 384), BF16), ((4, 16, 8, LANES), BF16)],

time: 131 us -> 136 us (1.038)
  blocking collectives: 0 us -> 38.5 us
  starting transfers between devices: 74.4 us -> 54.9 us
  waiting for transfers between devices: 38.4 us -> 25.5 us
    all_to_all x0 -> x1, blocking collectives: none -> 38.5 us  [exchange(): return lax.all_to_all(value, axis, split_axis=0, concat_axis=0, tiled=True)]
    ppermute x9, waiting for transfers between devices: 26.7 us -> 8.68 us  [shifted(): return lax.ppermute(value, SEQ, pairs)]
    all_to_all x2 -> x1, starting transfers between devices: 33.7 us -> 16.3 us  [exchange(): return lax.all_to_all(value, axis, split_axis=0, concat_axis=0, tiled=True)]
    ppermute x4, waiting for transfers between devices: 11.7 us -> 16.8 us  [turned(): lax.ppermute(value, axis, [(i, (i + by) % peers) for i in range(peers)])]
    ppermute x9, starting transfers between devices: 28.7 us -> 26.9 us  [shifted(): return lax.ppermute(value, SEQ, pairs)]
  transfers between devices with their start and end apart: 15 -> 14, of which waited for: 6 -> 6; matrix products, arithmetic and copies ran while one was open for 0% -> 0% of each run, Pallas kernels for 4% -> 4%
where the time goes in v4:
time: 136 us; the launch traced here: 135 us
  starting transfers between devices  54.9 us (40%)
  blocking collectives  38.5 us (28%)
  waiting for transfers between devices  25.5 us (19%)
  Pallas kernels  13.3 us (10%)
  local copies, waits for them, and re-layouts  1.43 us (1%)
    all_to_all x1, blocking collectives, exchange(): return lax.all_to_all(value, axis, split_axis=0, concat_axis=0, tiled=True)  38.5 us
    ppermute x9, starting transfers between devices, shifted(): return lax.ppermute(value, SEQ, pairs)  26.9 us
    ppermute x4, waiting for transfers between devices, turned(): lax.ppermute(value, axis, [(i, (i + by) % peers) for i in range(peers)])  16.8 us
    all_to_all x1, starting transfers between devices, exchange(): return lax.all_to_all(value, axis, split_axis=0, concat_axis=0, tiled=True)  16.3 us
    pallas_call x7, Pallas kernels, call(): pl.pallas_call(body, out_shape=[pltpu.HBM(s, t) if c == 'h' else jax.Shap...  13.3 us
    ppermute x4, starting transfers between devices, turned(): lax.ppermute(value, axis, [(i, (i + by) % peers) for i in range(peers)])  11.7 us
    ppermute x9, waiting for transfers between devices, shifted(): return lax.ppermute(value, SEQ, pairs)  8.68 us
  transfers between devices with their start and end apart: 14, of which 6 were waited for; matrix products, arithmetic and copies ran while one was open for 0% of the time, Pallas kernels for 4%

profile of v4, /device:TPU:7, one launch (start us, length us, event | category | flops | bytes accessed | tf_op | source)
XLA Modules:
  0.0 134.5 jit_solution(12403383640109042977)
XLA Ops:
  0.6 1.2 shard_map.103
  1.8 38.5 %all_to_all.10.got = bf16[16,104,128]{2,1,0:T(8,128)(2,1)S(1)} all-to-all(bf16[16,104,128]{2,1,0:T(8,128)(2,1)S(1)} %get-tuple-element.32), channel_id=1, replica_groups=mesh['z'=16,'x'=4,'core'=2,'head'=8] {'z'}, dimensions={0} | all-to-all | bytes 851968 | tf_op jit(solution)/shard_map/all_to_all | solution.py:35
  40.4 1.6 %shard_map.104 = (bf16[16,80,128]{2,1,0:T(8,128)(2,1)}, bf16[8,8,48,128]{3,2,1,0:T(8,128)(2,1)}) custom-call(bf16[16,104,128]{2,1,0:T(8,128)(2,1)S(1)} %all_to_all.10.got), custom_call_target="tpu_custom_call" | custom-call | flops 100000000 | bytes 1540096 | tf_op jit(solution)/shard_map/pallas_call | solution.py:53
  42.0 0.0 copy-start.8
  42.0 0.0 copy-start.4
  42.0 16.3 %all-to-all-start.1 = ((bf16[64,48,128]{2,1,0:T(8,128)(2,1)}), bf16[64,48,128]{2,1,0:T(8,128)(2,1)S(1)}, u32[]{:S(2)}, u32[]{:S(2)}) async-start(bf16[64,48,128]{2,1,0:T(8,128)(2,1)} %bitcast.4), calls=%async_computation.1 | async-start | bytes 1572864 | tf_op jit(solution)/shard_map/all_to_all | solution.py:35
  58.3 0.0 copy-done.8
  58.3 0.0 copy-start
  58.4 2.5 %collective-permute-start = (bf16[16,80,128]{2,1,0:T(8,128)(2,1)S(1)}, bf16[16,80,128]{2,1,0:T(8,128)(2,1)S(1)}, u32[]{:S(2)}, u32[]{:S(2)}) collective-permute-start(bf16[16,80,128]{2,1,0:T(8,128)(2,1)S(1)} %copy-done.8), channel_id=1, source_target_pairs={{0,48},{16,0},{32,16},{48,32},{1,49},{17,1},{33,17},{49,33},{2,50}... | collective-permute-start | bytes 983048 | tf_op jit(solution)/shard_map/ppermute | solution.py:31
  60.8 15.7 %collective-permute-done.o3 = bf16[16,80,128]{2,1,0:T(8,128)(2,1)S(1)} collective-permute-done((bf16[16,80,128]{2,1,0:T(8,128)(2,1)S(1)}, bf16[16,80,128]{2,1,0:T(8,128)(2,1)S(1)}, u32[]{:S(2)}, u32[]{:S(2)}) %collective-permute-start) | collective-permute-done | bytes 327712 | tf_op jit(solution)/shard_map/ppermute | solution.py:31
  76.5 0.0 copy-start.9
  76.5 1.9 %collective-permute-start.1 = (bf16[16,80,128]{2,1,0:T(8,128)(2,1)S(1)}, bf16[16,80,128]{2,1,0:T(8,128)(2,1)S(1)}, u32[]{:S(2)}, u32[]{:S(2)}) collective-permute-start(bf16[16,80,128]{2,1,0:T(8,128)(2,1)S(1)} %collective-permute-done.o3), channel_id=1, source_target_pairs={{0,48},{16,0},{32,16},{48,32},{1,49},{17,1},{33,17},{49,33},{2,50}... | collective-permute-start | bytes 983048 | tf_op jit(solution)/shard_map/ppermute | solution.py:31
  78.5 4.6 %collective-permute-start.8 = (bf16[16,80,128]{2,1,0:T(8,128)(2,1)S(1)}, bf16[16,80,128]{2,1,0:T(8,128)(2,1)S(1)}, u32[]{:S(2)}, u32[]{:S(2)}) collective-permute-start(bf16[16,80,128]{2,1,0:T(8,128)(2,1)S(1)} %copy-done.8), channel_id=1, source_target_pairs={{0,16},{16,32},{32,48},{48,0},{1,17},{17,33},{33,49},{49,1},{2,18}... | collective-permute-start | bytes 983048 | tf_op jit(solution)/shard_map/ppermute | solution.py:31
  83.0 0.0 copy-done.4
  83.1 1.9 %collective-permute-start.7 = (bf16[128,384]{1,0:T(8,128)(2,1)S(1)}, bf16[128,384]{1,0:T(8,128)(2,1)S(1)}, u32[]{:S(2)}, u32[]{:S(2)}) collective-permute-start(bf16[128,384]{1,0:T(8,128)(2,1)S(1)} %copy-done.4), channel_id=1, source_target_pairs={{32,0},{40,8},{48,16},{56,24},{64,32},{72,40},{80,48},{88,56},{96,... | collective-permute-start | bytes 294920 | tf_op jit(solution)/shard_map/ppermute | solution.py:26
  85.0 2.5 %collective-permute-start.6 = (bf16[128,384]{1,0:T(8,128)(2,1)S(1)}, bf16[128,384]{1,0:T(8,128)(2,1)S(1)}, u32[]{:S(2)}, u32[]{:S(2)}) collective-permute-start(bf16[128,384]{1,0:T(8,128)(2,1)S(1)} %copy-done.4), channel_id=1, source_target_pairs={{16,0},{24,8},{32,16},{40,24},{48,32},{56,40},{64,48},{72,56},{80,... | collective-permute-start | bytes 294920 | tf_op jit(solution)/shard_map/ppermute | solution.py:26
  87.5 3.5 %collective-permute-start.5 = (bf16[128,384]{1,0:T(8,128)(2,1)S(1)}, bf16[128,384]{1,0:T(8,128)(2,1)S(1)}, u32[]{:S(2)}, u32[]{:S(2)}) collective-permute-start(bf16[128,384]{1,0:T(8,128)(2,1)S(1)} %copy-done.4), channel_id=1, source_target_pairs={{8,0},{16,8},{24,16},{32,24},{40,32},{48,40},{56,48},{64,56},{72,6... | collective-permute-start | bytes 294920 | tf_op jit(solution)/shard_map/ppermute | solution.py:26
  91.0 0.0 collective-permute-done.7.l4
  91.0 0.0 copy-start.5
  91.1 5.2 %collective-permute-start.4 = (bf16[128,768]{1,0:T(8,128)(2,1)S(1)}, bf16[128,768]{1,0:T(8,128)(2,1)S(1)}, u32[]{:S(2)}, u32[]{:S(2)}) collective-permute-start(bf16[128,768]{1,0:T(8,128)(2,1)S(1)} %get-tuple-element.35), channel_id=1, source_target_pairs={{0,32},{8,40},{16,48},{24,56},{32,64},{40,72},{48,80},{56,88},{64,... | collective-permute-start | bytes 589832 | tf_op jit(solution)/shard_map/ppermute | solution.py:26
  96.3 0.0 collective-permute-done.6.l2
  96.3 0.0 copy-start.6
  96.3 4.2 %collective-permute-start.3 = (bf16[128,768]{1,0:T(8,128)(2,1)S(1)}, bf16[128,768]{1,0:T(8,128)(2,1)S(1)}, u32[]{:S(2)}, u32[]{:S(2)}) collective-permute-start(bf16[128,768]{1,0:T(8,128)(2,1)S(1)} %get-tuple-element.35), channel_id=1, source_target_pairs={{0,16},{8,24},{16,32},{24,40},{32,48},{40,56},{48,64},{56,72},{64,... | collective-permute-start | bytes 589832 | tf_op jit(solution)/shard_map/ppermute | solution.py:26
  100.5 0.0 collective-permute-done.5.l1
  100.5 0.0 copy-start.7
  100.6 2.2 %collective-permute-start.2 = (bf16[128,768]{1,0:T(8,128)(2,1)S(1)}, bf16[128,768]{1,0:T(8,128)(2,1)S(1)}, u32[]{:S(2)}, u32[]{:S(2)}) collective-permute-start(bf16[128,768]{1,0:T(8,128)(2,1)S(1)} %get-tuple-element.35), channel_id=1, source_target_pairs={{0,8},{8,16},{16,24},{24,32},{32,40},{40,48},{48,56},{56,64},{64,7... | collective-permute-start | bytes 589832 | tf_op jit(solution)/shard_map/ppermute | solution.py:26
  102.8 0.0 collective-permute-done.4.b4
  102.8 0.0 copy-start.1
  102.8 1.7 %collective-permute-done.3.b2 = bf16[128,768]{1,0:T(8,128)(2,1)S(1)} collective-permute-done((bf16[128,768]{1,0:T(8,128)(2,1)S(1)}, bf16[128,768]{1,0:T(8,128)(2,1)S(1)}, u32[]{:S(2)}, u32[]{:S(2)}) %collective-permute-start.3) | collective-permute-done | bytes 196640 | tf_op jit(solution)/shard_map/ppermute | solution.py:26
  104.5 0.0 copy-start.2
  104.5 2.9 %collective-permute-done.2.b1 = bf16[128,768]{1,0:T(8,128)(2,1)S(1)} collective-permute-done((bf16[128,768]{1,0:T(8,128)(2,1)S(1)}, bf16[128,768]{1,0:T(8,128)(2,1)S(1)}, u32[]{:S(2)}, u32[]{:S(2)}) %collective-permute-start.2) | collective-permute-done | bytes 196640 | tf_op jit(solution)/shard_map/ppermute | solution.py:26
  107.3 0.0 copy-done.5
  107.3 0.0 copy-done.6
  107.4 0.0 copy-done.7
  107.4 0.0 copy-done.1
  107.4 0.0 copy-done.2
  107.4 0.0 copy-start.3
  107.4 0.7 copy-done.3
  108.0 0.0 copy-done
  108.0 3.6 %shard_map.105 = (f32[3,512,128]{2,1,0:T(8,128)}, f32[8,384]{1,0:T(8,128)}, f32[9,128,128]{2,1,0:T(8,128)}) custom-call(s32[1]{0:T(128)} %bitcast.frame, s32[1,2]{1,0:T(1,128)S(1)} %copy-done, bf16[128,384]{1,0:T(8,128)(2,1)} %query_h.3, bf16[128,384]{1,0:T(8,128)(2,1)} %key_h.5, bf16[128,384]{1,0:T(8,128)(2,1)} %value_h.5, bf16[128,768]{1,0:T(8,128)(2,1)} %copy-done.3, ...), custom_call_target="tpu_custom_call" | custom-call | flops 90000000 | bytes 2568204 | tf_op jit(solution)/shard_map/pallas_call | solution.py:53
  111.7 0.0 collective-permute-done.1.o2
  111.7 0.0 copy-start.10
  111.7 0.0 all-to-all-done.1
  111.7 0.0 collective-permute-done.8.o1
  111.7 0.0 copy-done.9
  111.7 0.7 copy-done.10
  112.4 2.4 %shard_map.106 = (f32[152,384]{1,0:T(8,128)S(1)}, f32[152,384]{1,0:T(8,128)S(1)}, bf16[4,128,384]{2,1,0:T(8,128)(2,1)S(1)}, bf16[4,128,384]{2,1,0:T(8,128)(2,1)S...) custom-call(s32[1]{0:T(128)} %bitcast.frame, ...), custom_call_target="tpu_custom_call" | custom-call | flops 350000000 | bytes 7700484 | tf_op jit(solution)/shard_map/pallas_call | solution.py:53
  114.9 2.7 %collective-permute-start.9 = (f32[152,384]{1,0:T(8,128)S(1)}, f32[152,384]{1,0:T(8,128)S(1)}, u32[]{:S(2)}, u32[]{:S(2)}) collective-permute-start(f32[152,384]{1,0:T(8,128)S(1)} %get-tuple-element.46), channel_id=1, source_target_pairs={{0,8},{8,0},{1,9},{9,1},{2,10},{10,2},{3,11},{11,3},{4,12},{12,4},... | collective-permute-start | bytes 700424 | tf_op jit(solution)/shard_map/ppermute | solution.py:31
  117.6 1.1 collective-permute-done.9.other
  118.7 1.2 shard_map.107
  119.8 2.8 %collective-permute-start.12 = (bf16[136,384]{1,0:T(8,128)(2,1)S(1)}, bf16[136,384]{1,0:T(8,128)(2,1)S(1)}, u32[]{:S(2)}, u32[]{:S(2)}) collective-permute-start(bf16[136,384]{1,0:T(8,128)(2,1)S(1)} %get-tuple-element.50.parcel), channel_id=1, source_target_pairs={{32,0},{40,8},{48,16},{56,24},{64,32},{72,40},{80,48},{88,56},{96,... | collective-permute-start | bytes 313352 | tf_op jit(solution)/shard_map/ppermute | solution.py:26
  122.7 1.9 %collective-permute-start.11 = (bf16[136,384]{1,0:T(8,128)(2,1)S(1)}, bf16[136,384]{1,0:T(8,128)(2,1)S(1)}, u32[]{:S(2)}, u32[]{:S(2)}) collective-permute-start(bf16[136,384]{1,0:T(8,128)(2,1)S(1)} %get-tuple-element.50.parcel), channel_id=1, source_target_pairs={{16,0},{24,8},{32,16},{40,24},{48,32},{56,40},{64,48},{72,56},{80,... | collective-permute-start | bytes 313352 | tf_op jit(solution)/shard_map/ppermute | solution.py:26
  124.6 2.6 %collective-permute-start.10 = (bf16[136,384]{1,0:T(8,128)(2,1)S(1)}, bf16[136,384]{1,0:T(8,128)(2,1)S(1)}, u32[]{:S(2)}, u32[]{:S(2)}) collective-permute-start(bf16[136,384]{1,0:T(8,128)(2,1)S(1)} %get-tuple-element.50.parcel), channel_id=1, source_target_pairs={{8,0},{16,8},{24,16},{32,24},{40,32},{48,40},{56,48},{64,56},{72,6... | collective-permute-start | bytes 313352 | tf_op jit(solution)/shard_map/ppermute | solution.py:26
  127.2 2.0 %shard_map.108 = (bf16[128,384]{1,0:T(8,128)(2,1)}, f32[128,384]{1,0:T(8,128)S(1)}, f32[128,384]{1,0:T(8,128)S(1)}) custom-call(bf16[136,384]{1,0:T(8,128)(2,1)S(1)} %get-tuple-element.50.parcel, f32[8,384]{1,0:T(8,128)S(1)} %get-tuple-element.51.row_dot, f32[3,512,128]{2,1,0:T(8,128)S(1)} %get-tuple-element.48.prob, ...), custom_call_target="tpu_custom_call" | custom-call | flops 120000000 | bytes 2279424 | tf_op jit(solution)/shard_map/pallas_call | solution.py:53
  129.1 0.0 collective-permute-done.12.a4
  129.1 1.1 collective-permute-done.11.a2
  130.2 3.0 %collective-permute-done.10.a1 = bf16[136,384]{1,0:T(8,128)(2,1)S(1)} collective-permute-done((bf16[136,384]{1,0:T(8,128)(2,1)S(1)}, bf16[136,384]{1,0:T(8,128)(2,1)S(1)}, u32[]{:S(2)}, u32[]{:S(2)}) %collective-permute-start.10) | collective-permute-done | bytes 104480 | tf_op jit(solution)/shard_map/ppermute | solution.py:26
  133.2 1.3 shard_map.109
Async XLA Ops:
  42.0 16.3 %copy-start.8 = (bf16[16,80,128]{2,1,0:T(8,128)(2,1)S(1)}, bf16[16,80,128]{2,1,0:T(8,128)(2,1)}, u32[]{:S(2)}) copy-start(bf16[16,80,128]{2,1,0:T(8,128)(2,1)} %get-tuple-element.34.o0) | copy-start | bytes 983044
  42.0 41.0 %copy-start.4 = (bf16[128,384]{1,0:T(8,128)(2,1)S(1)}, bf16[128,384]{1,0:T(8,128)(2,1)}, u32[]{:S(2)}) copy-start(bf16[128,384]{1,0:T(8,128)(2,1)} %query_h.3) | copy-start | bytes 294916
  42.0 69.7 %all-to-all-start.1 = ((bf16[64,48,128]{2,1,0:T(8,128)(2,1)}), bf16[64,48,128]{2,1,0:T(8,128)(2,1)S(1)}, u32[]{:S(2)}, u32[]{:S(2)}) async-start(bf16[64,48,128]{2,1,0:T(8,128)(2,1)} %bitcast.4), calls=%async_computation.1 | async-start | bytes 1572864 | tf_op jit(solution)/shard_map/all_to_all | solution.py:35
  58.3 49.7 %copy-start = (s32[1,2]{1,0:T(1,128)S(1)}, s32[1,2]{1,0:T(1,128)}, u32[]{:S(2)}) copy-start(s32[1,2]{1,0:T(1,128)} %band.3) | copy-start | bytes 28
  58.4 18.2 %collective-permute-start = (bf16[16,80,128]{2,1,0:T(8,128)(2,1)S(1)}, bf16[16,80,128]{2,1,0:T(8,128)(2,1)S(1)}, u32[]{:S(2)}, u32[]{:S(2)}) collective-permute-start(bf16[16,80,128]{2,1,0:T(8,128)(2,1)S(1)} %copy-done.8), channel_id=1, source_target_pairs={{0,48},{16,0},{32,16},{48,32},{1,49},{17,1},{33,17},{49,33},{2,50}... | collective-permute-start | bytes 983048 | tf_op jit(solution)/shard_map/ppermute | solution.py:31
  76.5 35.2 %copy-start.9 = (bf16[16,80,128]{2,1,0:T(8,128)(2,1)}, bf16[16,80,128]{2,1,0:T(8,128)(2,1)S(1)}, u32[]{:S(2)}) copy-start(bf16[16,80,128]{2,1,0:T(8,128)(2,1)S(1)} %collective-permute-done.o3) | copy-start | bytes 983044
  76.5 35.1 %collective-permute-start.1 = (bf16[16,80,128]{2,1,0:T(8,128)(2,1)S(1)}, bf16[16,80,128]{2,1,0:T(8,128)(2,1)S(1)}, u32[]{:S(2)}, u32[]{:S(2)}) collective-permute-start(bf16[16,80,128]{2,1,0:T(8,128)(2,1)S(1)} %collective-permute-done.o3), channel_id=1, source_target_pairs={{0,48},{16,0},{32,16},{48,32},{1,49},{17,1},{33,17},{49,33},{2,50}... | collective-permute-start | bytes 983048 | tf_op jit(solution)/shard_map/ppermute | solution.py:31
  78.5 33.2 %collective-permute-start.8 = (bf16[16,80,128]{2,1,0:T(8,128)(2,1)S(1)}, bf16[16,80,128]{2,1,0:T(8,128)(2,1)S(1)}, u32[]{:S(2)}, u32[]{:S(2)}) collective-permute-start(bf16[16,80,128]{2,1,0:T(8,128)(2,1)S(1)} %copy-done.8), channel_id=1, source_target_pairs={{0,16},{16,32},{32,48},{48,0},{1,17},{17,33},{33,49},{49,1},{2,18}... | collective-permute-start | bytes 983048 | tf_op jit(solution)/shard_map/ppermute | solution.py:31
  83.1 8.0 %collective-permute-start.7 = (bf16[128,384]{1,0:T(8,128)(2,1)S(1)}, bf16[128,384]{1,0:T(8,128)(2,1)S(1)}, u32[]{:S(2)}, u32[]{:S(2)}) collective-permute-start(bf16[128,384]{1,0:T(8,128)(2,1)S(1)} %copy-done.4), channel_id=1, source_target_pairs={{32,0},{40,8},{48,16},{56,24},{64,32},{72,40},{80,48},{88,56},{96,... | collective-permute-start | bytes 294920 | tf_op jit(solution)/shard_map/ppermute | solution.py:26
  85.0 11.3 %collective-permute-start.6 = (bf16[128,384]{1,0:T(8,128)(2,1)S(1)}, bf16[128,384]{1,0:T(8,128)(2,1)S(1)}, u32[]{:S(2)}, u32[]{:S(2)}) collective-permute-start(bf16[128,384]{1,0:T(8,128)(2,1)S(1)} %copy-done.4), channel_id=1, source_target_pairs={{16,0},{24,8},{32,16},{40,24},{48,32},{56,40},{64,48},{72,56},{80,... | collective-permute-start | bytes 294920 | tf_op jit(solution)/shard_map/ppermute | solution.py:26
  87.5 13.1 %collective-permute-start.5 = (bf16[128,384]{1,0:T(8,128)(2,1)S(1)}, bf16[128,384]{1,0:T(8,128)(2,1)S(1)}, u32[]{:S(2)}, u32[]{:S(2)}) collective-permute-start(bf16[128,384]{1,0:T(8,128)(2,1)S(1)} %copy-done.4), channel_id=1, source_target_pairs={{8,0},{16,8},{24,16},{32,24},{40,32},{48,40},{56,48},{64,56},{72,6... | collective-permute-start | bytes 294920 | tf_op jit(solution)/shard_map/ppermute | solution.py:26
  91.0 16.3 %copy-start.5 = (bf16[128,384]{1,0:T(8,128)(2,1)}, bf16[128,384]{1,0:T(8,128)(2,1)S(1)}, u32[]{:S(2)}) copy-start(bf16[128,384]{1,0:T(8,128)(2,1)S(1)} %collective-permute-done.7.l4) | copy-start | bytes 294916
  91.1 11.7 %collective-permute-start.4 = (bf16[128,768]{1,0:T(8,128)(2,1)S(1)}, bf16[128,768]{1,0:T(8,128)(2,1)S(1)}, u32[]{:S(2)}, u32[]{:S(2)}) collective-permute-start(bf16[128,768]{1,0:T(8,128)(2,1)S(1)} %get-tuple-element.35), channel_id=1, source_target_pairs={{0,32},{8,40},{16,48},{24,56},{32,64},{40,72},{48,80},{56,88},{64,... | collective-permute-start | bytes 589832 | tf_op jit(solution)/shard_map/ppermute | solution.py:26
  96.3 11.1 %copy-start.6 = (bf16[128,384]{1,0:T(8,128)(2,1)}, bf16[128,384]{1,0:T(8,128)(2,1)S(1)}, u32[]{:S(2)}) copy-start(bf16[128,384]{1,0:T(8,128)(2,1)S(1)} %collective-permute-done.6.l2) | copy-start | bytes 294916
  96.3 8.2 %collective-permute-start.3 = (bf16[128,768]{1,0:T(8,128)(2,1)S(1)}, bf16[128,768]{1,0:T(8,128)(2,1)S(1)}, u32[]{:S(2)}, u32[]{:S(2)}) collective-permute-start(bf16[128,768]{1,0:T(8,128)(2,1)S(1)} %get-tuple-element.35), channel_id=1, source_target_pairs={{0,16},{8,24},{16,32},{24,40},{32,48},{40,56},{48,64},{56,72},{64,... | collective-permute-start | bytes 589832 | tf_op jit(solution)/shard_map/ppermute | solution.py:26
  100.5 6.8 %copy-start.7 = (bf16[128,384]{1,0:T(8,128)(2,1)}, bf16[128,384]{1,0:T(8,128)(2,1)S(1)}, u32[]{:S(2)}) copy-start(bf16[128,384]{1,0:T(8,128)(2,1)S(1)} %collective-permute-done.5.l1) | copy-start | bytes 294916
  100.6 6.8 %collective-permute-start.2 = (bf16[128,768]{1,0:T(8,128)(2,1)S(1)}, bf16[128,768]{1,0:T(8,128)(2,1)S(1)}, u32[]{:S(2)}, u32[]{:S(2)}) collective-permute-start(bf16[128,768]{1,0:T(8,128)(2,1)S(1)} %get-tuple-element.35), channel_id=1, source_target_pairs={{0,8},{8,16},{16,24},{24,32},{32,40},{40,48},{48,56},{56,64},{64,7... | collective-permute-start | bytes 589832 | tf_op jit(solution)/shard_map/ppermute | solution.py:26
  102.8 4.6 %copy-start.1 = (bf16[128,768]{1,0:T(8,128)(2,1)}, bf16[128,768]{1,0:T(8,128)(2,1)S(1)}, u32[]{:S(2)}) copy-start(bf16[128,768]{1,0:T(8,128)(2,1)S(1)} %collective-permute-done.4.b4) | copy-start | bytes 589828
  104.5 2.9 %copy-start.2 = (bf16[128,768]{1,0:T(8,128)(2,1)}, bf16[128,768]{1,0:T(8,128)(2,1)S(1)}, u32[]{:S(2)}) copy-start(bf16[128,768]{1,0:T(8,128)(2,1)S(1)} %collective-permute-done.3.b2) | copy-start | bytes 589828
  107.4 0.7 copy-start.3
  111.7 0.8 copy-start.10
  114.9 3.8 %collective-permute-start.9 = (f32[152,384]{1,0:T(8,128)S(1)}, f32[152,384]{1,0:T(8,128)S(1)}, u32[]{:S(2)}, u32[]{:S(2)}) collective-permute-start(f32[152,384]{1,0:T(8,128)S(1)} %get-tuple-element.46), channel_id=1, source_target_pairs={{0,8},{8,0},{1,9},{9,1},{2,10},{10,2},{3,11},{11,3},{4,12},{12,4},... | collective-permute-start | bytes 700424 | tf_op jit(solution)/shard_map/ppermute | solution.py:31
  119.8 9.3 %collective-permute-start.12 = (bf16[136,384]{1,0:T(8,128)(2,1)S(1)}, bf16[136,384]{1,0:T(8,128)(2,1)S(1)}, u32[]{:S(2)}, u32[]{:S(2)}) collective-permute-start(bf16[136,384]{1,0:T(8,128)(2,1)S(1)} %get-tuple-element.50.parcel), channel_id=1, source_target_pairs={{32,0},{40,8},{48,16},{56,24},{64,32},{72,40},{80,48},{88,56},{96,... | collective-permute-start | bytes 313352 | tf_op jit(solution)/shard_map/ppermute | solution.py:26
  122.7 7.5 %collective-permute-start.11 = (bf16[136,384]{1,0:T(8,128)(2,1)S(1)}, bf16[136,384]{1,0:T(8,128)(2,1)S(1)}, u32[]{:S(2)}, u32[]{:S(2)}) collective-permute-start(bf16[136,384]{1,0:T(8,128)(2,1)S(1)} %get-tuple-element.50.parcel), channel_id=1, source_target_pairs={{16,0},{24,8},{32,16},{40,24},{48,32},{56,40},{64,48},{72,56},{80,... | collective-permute-start | bytes 313352 | tf_op jit(solution)/shard_map/ppermute | solution.py:26
  124.6 8.7 %collective-permute-start.10 = (bf16[136,384]{1,0:T(8,128)(2,1)S(1)}, bf16[136,384]{1,0:T(8,128)(2,1)S(1)}, u32[]{:S(2)}, u32[]{:S(2)}) collective-permute-start(bf16[136,384]{1,0:T(8,128)(2,1)S(1)} %get-tuple-element.50.parcel), channel_id=1, source_target_pairs={{8,0},{16,8},{24,16},{32,24},{40,32},{48,40},{56,48},{64,56},{72,6... | collective-permute-start | bytes 313352 | tf_op jit(solution)/shard_map/ppermute | solution.py:26
